TPU v7x, 512 devices: a whole 4x4x16 slice. The times are simulated.
512 devices in a mesh: patch: 64 (over z, y_lo, core), band: 8 (over x, y_hi).
Axes of the slice: x: 4, y: 4 (y_hi: 2, y_lo: 2; y = y_hi * 2 + y_lo), z: 16, core: 2. Of those that a mesh axis runs over, the one named last changes fastest.
Arguments:
- tile_flux: bfloat16 [6, 8192, 8, 128], P(None, ('patch', 'band')), may hold values from -6 to 6
- tile_weight: bfloat16 [6, 8192, 8, 128], P(None, ('patch', 'band')), may hold values from 0.19921875 to 5
- dest_patch: int32 [6, 8192], P(None, ('patch', 'band')), may hold values from 0 to 63, as said below
- dest_block: int32 [6, 8192], P(None, ('patch', 'band')), may hold values from 0 to 15, as said below
- basis: bfloat16 [2, 21, 31], replicated, may hold values from -1 to 1
- spatial: float32 [64, 6, 3, 21], P('patch'), may hold values from -1.25 to 1.25
Outputs:
- coadd: float32 [64, 256, 512], P('patch', 'band')
Inputs may be any that keep to these rules, and one draw needn't show every extreme that they name: `dest_patch`: for each visit, the tiles held by one device go to exactly 8 different patches, 2 tiles to each. `dest_block`: for each visit, every block of every band of every patch receives exactly one tile.
All inputs are finite; a program needn't handle non-finite values.
Results may differ from a plain program's by a relative error of at most 0.0029.
Values may be sent and summed in bfloat16 or wider, within the bound.
A program may use at most 64 MiB of HBM per device.

v0:
```python
import jax
import jax.numpy as jnp
from jax import lax
from jax.sharding import PartitionSpec as P

BASIS = 21
TAPS = 31
ROWS = 32
COLS = 512
CAP = 2


def extended(value, sides, width):
    for axis, dim in sides:
        count, length = (lax.axis_size(axis), value.shape[dim])
        up = [(i, (i + 1) % count) for i in range(count - 1)]
        down = [(j, i) for i, j in up]
        last = lax.slice_in_dim(value, length - width, length, axis=dim)
        leading = lax.slice_in_dim(value, 0, width, axis=dim)
        before = lax.ppermute(last, axis, up)
        after = lax.ppermute(leading, axis, down)
        value = jnp.concatenate([before, value, after], axis=dim)
    return value


def column_table(basis):
    width = 128 + TAPS - 1
    inner = jnp.arange(width)[:, None, None]
    outer = jnp.arange(128)[None, :, None]
    offset = jnp.arange(TAPS)[None, None, :]
    ones = (inner - outer == offset).astype(jnp.float32)
    table = jnp.einsum("iot,bt->ibo", ones, basis[0].astype(jnp.float32))
    return table.reshape(width, BASIS * 128).astype(jnp.bfloat16)


def row_table(basis):
    target = jnp.arange(ROWS)[:, None, None]
    source = jnp.arange(ROWS + TAPS - 1)[None, :, None]
    offset = jnp.arange(TAPS)[None, None, :]
    ones = (source - target == offset).astype(jnp.float32)
    table = jnp.einsum("stk,bk->bst", ones, basis[1].astype(jnp.float32))
    return table.astype(jnp.bfloat16)


def column_filter(rows_block, table):
    margin = TAPS // 2
    padded = jnp.pad(rows_block, ((0, 0), (margin, margin)))
    pieces = jnp.stack(
        [padded[:, 128 * column : 128 * column + 128 + TAPS - 1] for column in range(COLS // 128)],
        axis=1,
    )
    result = jnp.einsum("rci,in->rcn", pieces, table, preferred_element_type=jnp.float32)
    return result.astype(jnp.bfloat16).reshape(rows_block.shape[0], COLS // 128, BASIS, 128)


def per_device(tile_flux, tile_weight, dest_patch, dest_block, basis, spatial):
    visits, tile_count, tile_height, tile_width = tile_flux.shape
    patches = lax.axis_size("patch")
    slot_count = patches * CAP
    pixels = tile_height * tile_width
    margin = TAPS // 2
    earlier = jnp.arange(tile_count)[None, :] < jnp.arange(tile_count)[:, None]
    matches = dest_patch[:, :, None] == dest_patch[:, None, :]
    ordinal = jnp.sum(jnp.logical_and(matches, earlier[None]), axis=2)
    slot_index = dest_patch * CAP + ordinal
    routing = slot_index[:, None, :] == jnp.arange(slot_count)[None, :, None]
    routing_b = routing.astype(jnp.bfloat16)
    send_flux = jnp.einsum(
        "vnt,vtx->vnx",
        routing_b,
        tile_flux.reshape(visits, tile_count, pixels),
        preferred_element_type=jnp.float32,
    )
    send_flux = send_flux.astype(jnp.bfloat16).reshape(
        visits, patches, CAP, tile_height, tile_width
    )
    send_weight = jnp.einsum(
        "vnt,vtx->vnx",
        routing_b,
        tile_weight.reshape(visits, tile_count, pixels),
        preferred_element_type=jnp.float32,
    )
    send_weight = send_weight.astype(jnp.bfloat16).reshape(
        visits, patches, CAP, tile_height, tile_width
    )
    send_block = jnp.sum(jnp.where(routing, dest_block[:, None, :] + 1, 0), axis=2) - 1
    send_block = send_block.astype(jnp.bfloat16).reshape(visits, patches, CAP)
    block_ids = jnp.arange(tile_count).astype(jnp.bfloat16)
    across = COLS // tile_width
    ctable = column_table(basis)
    rtable = row_table(basis)
    patch_rows = ROWS * lax.axis_size("band")
    first_row = (lax.axis_index("band") * ROWS).astype(jnp.float32)
    row_coord = (2.0 * (first_row + jnp.arange(ROWS, dtype=jnp.float32)) + 1.0) / patch_rows - 1.0
    col_coord = ((2.0 * jnp.arange(COLS, dtype=jnp.float32) + 1.0) / COLS - 1.0).reshape(
        COLS // 128, 128
    )

    def one_visit(inputs):
        flux_k, weight_k, block_k, spatial_row = inputs
        placing = (block_k.reshape(slot_count)[None, :] == block_ids[:, None]).astype(jnp.bfloat16)
        placed = jnp.dot(
            placing, flux_k.reshape(slot_count, pixels), preferred_element_type=jnp.float32
        )
        placed_weight = jnp.dot(
            placing, weight_k.reshape(slot_count, pixels), preferred_element_type=jnp.float32
        )
        frame = placed.astype(jnp.bfloat16).reshape(
            ROWS // tile_height, across, tile_height, tile_width
        )
        frame = frame.transpose(0, 2, 1, 3).reshape(ROWS, COLS)
        weight_frame = placed_weight.reshape(ROWS // tile_height, across, tile_height, tile_width)
        weight_frame = weight_frame.transpose(0, 2, 1, 3).reshape(ROWS, COLS)
        widened = extended(frame, (("band", 0),), margin)
        filtered = column_filter(widened, ctable)
        smoothed = jnp.einsum(
            "bst,tcbo->scbo", rtable, filtered, preferred_element_type=jnp.float32
        )
        mixture = jnp.einsum(
            "scbo,jb->jsco",
            smoothed,
            spatial_row,
            precision=lax.Precision.HIGHEST,
            preferred_element_type=jnp.float32,
        )
        matched = mixture[0] + row_coord[:, None, None] * mixture[1] + col_coord[None] * mixture[2]
        matched = matched.reshape(ROWS, COLS)
        return (weight_frame * matched, weight_frame)

    flux_in, weight_in, block_in = (
        lax.all_to_all(send_flux, "patch", split_axis=1, concat_axis=1, tiled=True),
        lax.all_to_all(send_weight, "patch", split_axis=1, concat_axis=1, tiled=True),
        lax.all_to_all(send_block, "patch", split_axis=1, concat_axis=1, tiled=True),
    )
    weighted, weight_sums = lax.map(one_visit, (flux_in, weight_in, block_in, spatial[0]))
    numerator = jnp.sum(weighted, axis=0)
    denominator = jnp.sum(weight_sums, axis=0)
    coadd = numerator / denominator
    return coadd[None]


def solution(mesh):
    in_specs = (
        P(None, ("patch", "band"), None, None),
        P(None, ("patch", "band"), None, None),
        P(None, ("patch", "band")),
        P(None, ("patch", "band")),
        P(),
        P("patch", None, None, None),
    )
    out_specs = P("patch", "band", None)
    return jax.shard_map(
        per_device, mesh=mesh, in_specs=in_specs, out_specs=out_specs, check_vma=False
    )
```

profile of v0, /device:TPU:6, one launch (start us, length us, event | category | flops | bytes accessed | tf_op | source)
XLA Modules:
  0.0 313.8 jit_solution(3637243762440474473)
XLA Ops:
  2.6 17.1 %all-to-all-start = ((bf16[6,64,2]{0,2,1:T(2,128)(2,1)}), bf16[6,64,2]{0,2,1:T(2,128)(2,1)S(1)}, u32[]{:S(2)}, u32[]{:S(2)}) async-start(bf16[6,64,2]{0,2,1:T(2,128)(2,1)} %bitcast), calls=%async_computation | async-start | bytes 65536 | tf_op jit(solution)/shard_map/all_to_all | solution.py:133
  23.7 9.4 %all-to-all-done = bf16[6,64,2]{0,2,1:T(2,128)(2,1)S(1)} async-done(((bf16[6,64,2]{0,2,1:T(2,128)(2,1)}), bf16[6,64,2]{0,2,1:T(2,128)(2,1)S(1)}, u32[]{:S(2)}, u32[]{:S(2)}) %all-to-all-start) | async-done | bytes 1568 | tf_op jit(solution)/shard_map/all_to_all | solution.py:133
  33.0 4.7 %all-to-all-start.1 = ((bf16[6,64,2,8,128]{4,3,2,0,1:T(8,128)(2,1)}), bf16[6,64,2,8,128]{4,3,2,0,1:T(8,128)(2,1)S(1)}, u32[]{:S(2)}, u32[]{:S(2)}) async-start(bf16[6,64,2,8,128]{4,3,2,0,1:T(8,128)(2,1)} %copy.32), calls=%async_computation.1 | async-start | bytes 3145728 | tf_op jit(solution)/shard_map/all_to_all | solution.py:132
  40.7 74.5 %all-to-all-done.1 = bf16[6,64,2,8,128]{4,3,2,0,1:T(8,128)(2,1)S(1)} async-done(((bf16[6,64,2,8,128]{4,3,2,0,1:T(8,128)(2,1)}), bf16[6,64,2,8,128]{4,3,2,0,1:T(8,128)(2,1)S(1)}, u32[]{:S(2)}, u32[]{:S(2)}) %all-to-all-start.1) | async-done | bytes 1572896 | tf_op jit(solution)/shard_map/all_to_all | solution.py:132
  115.3 5.7 %all-to-all-start.2 = ((bf16[6,64,2,8,128]{4,3,2,0,1:T(8,128)(2,1)}), bf16[6,64,2,8,128]{4,3,2,0,1:T(8,128)(2,1)}, u32[]{:S(2)}, u32[]{:S(2)}) async-start(bf16[6,64,2,8,128]{4,3,2,0,1:T(8,128)(2,1)} %copy.33), calls=%async_computation.2 | async-start | bytes 3145728 | tf_op jit(solution)/shard_map/all_to_all | solution.py:131
  123.6 74.8 %all-to-all-done.2 = bf16[6,64,2,8,128]{4,3,2,0,1:T(8,128)(2,1)} async-done(((bf16[6,64,2,8,128]{4,3,2,0,1:T(8,128)(2,1)}), bf16[6,64,2,8,128]{4,3,2,0,1:T(8,128)(2,1)}, u32[]{:S(2)}, u32[]{:S(2)}) %all-to-all-start.2) | async-done | bytes 1572896 | tf_op jit(solution)/shard_map/all_to_all | solution.py:131
  198.4 113.7 %while.16 = (s32[]{:T(128)}, f32[6,32,512]{2,1,0:T(8,128)S(1)}, f32[6,32,512]{2,1,0:T(8,128)}, bf16[6,64,2]{2,1,0:T(8,128)(2,1)}, bf16[6,64,2,8,128]{4,3,2,0,1:T...) while((s32[]{:T(128)}, f32[6,32,512]{2,1,0:T(8,128)S(1)}, ...), condition=%wide.region_3.4_spmd.clone.clone, body=%wide.region_2.3_spmd.clone.clone.sunk | while | flops 275175392 | bytes 33296936 | solution.py:135
  200.5 5.1 %collective-permute-start = (bf16[15,512]{1,0:T(8,128)(2,1)S(1)}, bf16[15,512]{1,0:T(8,128)(2,1)S(1)}, u32[]{:S(2)}, u32[]{:S(2)}) collective-permute-start(bf16[15,512]{1,0:T(8,128)(2,1)S(1)} %get-tuple-element.366), channel_id=1, source_target_pairs={{1,0},{2,1},{3,2},{4,3},{5,4},{6,5},{7,6},{9,8},{10,9},{11,10},{12... | collective-permute-start | bytes 46088 | tf_op jit(solution)/shard_map/while/body/eval_jaxpr/ppermute | solution.py:21
  205.6 2.3 collective-permute-start.1
  208.5 5.1 %collective-permute-done.1 = bf16[15,512]{1,0:T(8,128)(2,1)S(1)} collective-permute-done((bf16[15,512]{1,0:T(8,128)(2,1)S(1)}, bf16[15,512]{1,0:T(8,128)(2,1)S(1)}, u32[]{:S(2)}, u32[]{:S(2)}) %collective-permute-start.1) | collective-permute-done | bytes 15392 | tf_op jit(solution)/shard_map/while/body/eval_jaxpr/ppermute | solution.py:20
  215.7 2.1 fusion.74
  223.2 5.4 %collective-permute-start.1 = (bf16[15,512]{1,0:T(8,128)(2,1)S(1)}, bf16[15,512]{1,0:T(8,128)(2,1)S(1)}, u32[]{:S(2)}, u32[]{:S(2)}) collective-permute-start(bf16[15,512]{1,0:T(8,128)(2,1)S(1)} %get-tuple-element.367), channel_id=1, source_target_pairs={{0,1},{1,2},{2,3},{3,4},{4,5},{5,6},{6,7},{8,9},{9,10},{10,11},{11... | collective-permute-start | bytes 46088 | tf_op jit(solution)/shard_map/while/body/eval_jaxpr/ppermute | solution.py:20
  233.3 2.1 fusion.74
  238.8 4.5 %collective-permute-start = (bf16[15,512]{1,0:T(8,128)(2,1)S(1)}, bf16[15,512]{1,0:T(8,128)(2,1)S(1)}, u32[]{:S(2)}, u32[]{:S(2)}) collective-permute-start(bf16[15,512]{1,0:T(8,128)(2,1)S(1)} %get-tuple-element.366), channel_id=1, source_target_pairs={{1,0},{2,1},{3,2},{4,3},{5,4},{6,5},{7,6},{9,8},{10,9},{11,10},{12... | collective-permute-start | bytes 46088 | tf_op jit(solution)/shard_map/while/body/eval_jaxpr/ppermute | solution.py:21
  243.3 2.8 collective-permute-start.1
  246.8 4.6 %collective-permute-done.1 = bf16[15,512]{1,0:T(8,128)(2,1)S(1)} collective-permute-done((bf16[15,512]{1,0:T(8,128)(2,1)S(1)}, bf16[15,512]{1,0:T(8,128)(2,1)S(1)}, u32[]{:S(2)}, u32[]{:S(2)}) %collective-permute-start.1) | collective-permute-done | bytes 15392 | tf_op jit(solution)/shard_map/while/body/eval_jaxpr/ppermute | solution.py:20
  253.4 2.1 fusion.74
  260.9 5.4 %collective-permute-start.1 = (bf16[15,512]{1,0:T(8,128)(2,1)S(1)}, bf16[15,512]{1,0:T(8,128)(2,1)S(1)}, u32[]{:S(2)}, u32[]{:S(2)}) collective-permute-start(bf16[15,512]{1,0:T(8,128)(2,1)S(1)} %get-tuple-element.367), channel_id=1, source_target_pairs={{0,1},{1,2},{2,3},{3,4},{4,5},{5,6},{6,7},{8,9},{9,10},{10,11},{11... | collective-permute-start | bytes 46088 | tf_op jit(solution)/shard_map/while/body/eval_jaxpr/ppermute | solution.py:20
  271.0 2.1 fusion.74
  276.6 4.5 %collective-permute-start = (bf16[15,512]{1,0:T(8,128)(2,1)S(1)}, bf16[15,512]{1,0:T(8,128)(2,1)S(1)}, u32[]{:S(2)}, u32[]{:S(2)}) collective-permute-start(bf16[15,512]{1,0:T(8,128)(2,1)S(1)} %get-tuple-element.366), channel_id=1, source_target_pairs={{1,0},{2,1},{3,2},{4,3},{5,4},{6,5},{7,6},{9,8},{10,9},{11,10},{12... | collective-permute-start | bytes 46088 | tf_op jit(solution)/shard_map/while/body/eval_jaxpr/ppermute | solution.py:21
  281.1 2.9 collective-permute-start.1
  284.5 4.6 %collective-permute-done.1 = bf16[15,512]{1,0:T(8,128)(2,1)S(1)} collective-permute-done((bf16[15,512]{1,0:T(8,128)(2,1)S(1)}, bf16[15,512]{1,0:T(8,128)(2,1)S(1)}, u32[]{:S(2)}, u32[]{:S(2)}) %collective-permute-start.1) | collective-permute-done | bytes 15392 | tf_op jit(solution)/shard_map/while/body/eval_jaxpr/ppermute | solution.py:20
  298.6 5.4 %collective-permute-start.1 = (bf16[15,512]{1,0:T(8,128)(2,1)S(1)}, bf16[15,512]{1,0:T(8,128)(2,1)S(1)}, u32[]{:S(2)}, u32[]{:S(2)}) collective-permute-start(bf16[15,512]{1,0:T(8,128)(2,1)S(1)} %get-tuple-element.367), channel_id=1, source_target_pairs={{0,1},{1,2},{2,3},{3,4},{4,5},{5,6},{6,7},{8,9},{9,10},{10,11},{11... | collective-permute-start | bytes 46088 | tf_op jit(solution)/shard_map/while/body/eval_jaxpr/ppermute | solution.py:20
  308.7 2.1 fusion.74
  (240 shorter events, 63.4 us)
Async XLA Ops:
  2.6 30.4 %all-to-all-start = ((bf16[6,64,2]{0,2,1:T(2,128)(2,1)}), bf16[6,64,2]{0,2,1:T(2,128)(2,1)S(1)}, u32[]{:S(2)}, u32[]{:S(2)}) async-start(bf16[6,64,2]{0,2,1:T(2,128)(2,1)} %bitcast), calls=%async_computation | async-start | bytes 65536 | tf_op jit(solution)/shard_map/all_to_all | solution.py:133
  23.7 14.0 %copy-start.4 = (bf16[6,16,8,128]{3,2,1,0:T(8,128)(2,1)S(1)}, bf16[6,16,8,128]{3,2,1,0:T(8,128)(2,1)}, u32[]{:S(2)}) copy-start(bf16[6,16,8,128]{3,2,1,0:T(8,128)(2,1)} %param.8) | copy-start | bytes 589828
  33.0 82.2 %all-to-all-start.1 = ((bf16[6,64,2,8,128]{4,3,2,0,1:T(8,128)(2,1)}), bf16[6,64,2,8,128]{4,3,2,0,1:T(8,128)(2,1)S(1)}, u32[]{:S(2)}, u32[]{:S(2)}) async-start(bf16[6,64,2,8,128]{4,3,2,0,1:T(8,128)(2,1)} %copy.32), calls=%async_computation.1 | async-start | bytes 3145728 | tf_op jit(solution)/shard_map/all_to_all | solution.py:132
  40.7 80.3 %copy-start.6 = (f32[1,6,3,21]{3,0,2,1:T(1,128)S(1)}, f32[1,6,3,21]{3,0,2,1:T(1,128)}, u32[]{:S(2)}) copy-start(f32[1,6,3,21]{3,0,2,1:T(1,128)} %param.13) | copy-start | bytes 4540
  40.7 80.3 %copy-start.5 = (bf16[2,21,31]{2,0,1:T(2,128)(2,1)S(1)}, bf16[2,21,31]{2,0,1:T(2,128)(2,1)}, u32[]{:S(2)}) copy-start(bf16[2,21,31]{2,0,1:T(2,128)(2,1)} %param.12) | copy-start | bytes 7816
  115.3 83.1 %all-to-all-start.2 = ((bf16[6,64,2,8,128]{4,3,2,0,1:T(8,128)(2,1)}), bf16[6,64,2,8,128]{4,3,2,0,1:T(8,128)(2,1)}, u32[]{:S(2)}, u32[]{:S(2)}) async-start(bf16[6,64,2,8,128]{4,3,2,0,1:T(8,128)(2,1)} %copy.33), calls=%async_computation.2 | async-start | bytes 3145728 | tf_op jit(solution)/shard_map/all_to_all | solution.py:131
  198.4 15.4 %copy-start = (bf16[158,2688]{1,0:T(8,128)(2,1)}, bf16[158,2688]{1,0:T(8,128)(2,1)S(1)}, u32[]{:S(2)}) copy-start(bf16[158,2688]{1,0:T(8,128)(2,1)S(1)} %get-tuple-element.406) | copy-start | bytes 2548228 | tf_op jit(solution)/shard_map/while
  200.5 8.0 %collective-permute-start = (bf16[15,512]{1,0:T(8,128)(2,1)S(1)}, bf16[15,512]{1,0:T(8,128)(2,1)S(1)}, u32[]{:S(2)}, u32[]{:S(2)}) collective-permute-start(bf16[15,512]{1,0:T(8,128)(2,1)S(1)} %get-tuple-element.366), channel_id=1, source_target_pairs={{1,0},{2,1},{3,2},{4,3},{5,4},{6,5},{7,6},{9,8},{10,9},{11,10},{12... | collective-permute-start | bytes 46088 | tf_op jit(solution)/shard_map/while/body/eval_jaxpr/ppermute | solution.py:21
  205.6 8.0 %collective-permute-start.1 = (bf16[15,512]{1,0:T(8,128)(2,1)S(1)}, bf16[15,512]{1,0:T(8,128)(2,1)S(1)}, u32[]{:S(2)}, u32[]{:S(2)}) collective-permute-start(bf16[15,512]{1,0:T(8,128)(2,1)S(1)} %get-tuple-element.367), channel_id=1, source_target_pairs={{0,1},{1,2},{2,3},{3,4},{4,5},{5,6},{6,7},{8,9},{9,10},{10,11},{11... | collective-permute-start | bytes 46088 | tf_op jit(solution)/shard_map/while/body/eval_jaxpr/ppermute | solution.py:20
  219.1 12.3 %copy-start = (bf16[158,2688]{1,0:T(8,128)(2,1)}, bf16[158,2688]{1,0:T(8,128)(2,1)S(1)}, u32[]{:S(2)}) copy-start(bf16[158,2688]{1,0:T(8,128)(2,1)S(1)} %get-tuple-element.406) | copy-start | bytes 2548228 | tf_op jit(solution)/shard_map/while
  221.3 8.0 %collective-permute-start = (bf16[15,512]{1,0:T(8,128)(2,1)S(1)}, bf16[15,512]{1,0:T(8,128)(2,1)S(1)}, u32[]{:S(2)}, u32[]{:S(2)}) collective-permute-start(bf16[15,512]{1,0:T(8,128)(2,1)S(1)} %get-tuple-element.366), channel_id=1, source_target_pairs={{1,0},{2,1},{3,2},{4,3},{5,4},{6,5},{7,6},{9,8},{10,9},{11,10},{12... | collective-permute-start | bytes 46088 | tf_op jit(solution)/shard_map/while/body/eval_jaxpr/ppermute | solution.py:21
  223.2 8.0 %collective-permute-start.1 = (bf16[15,512]{1,0:T(8,128)(2,1)S(1)}, bf16[15,512]{1,0:T(8,128)(2,1)S(1)}, u32[]{:S(2)}, u32[]{:S(2)}) collective-permute-start(bf16[15,512]{1,0:T(8,128)(2,1)S(1)} %get-tuple-element.367), channel_id=1, source_target_pairs={{0,1},{1,2},{2,3},{3,4},{4,5},{5,6},{6,7},{8,9},{9,10},{10,11},{11... | collective-permute-start | bytes 46088 | tf_op jit(solution)/shard_map/while/body/eval_jaxpr/ppermute | solution.py:20
  236.6 14.9 %copy-start = (bf16[158,2688]{1,0:T(8,128)(2,1)}, bf16[158,2688]{1,0:T(8,128)(2,1)S(1)}, u32[]{:S(2)}) copy-start(bf16[158,2688]{1,0:T(8,128)(2,1)S(1)} %get-tuple-element.406) | copy-start | bytes 2548228 | tf_op jit(solution)/shard_map/while
  238.8 8.0 %collective-permute-start = (bf16[15,512]{1,0:T(8,128)(2,1)S(1)}, bf16[15,512]{1,0:T(8,128)(2,1)S(1)}, u32[]{:S(2)}, u32[]{:S(2)}) collective-permute-start(bf16[15,512]{1,0:T(8,128)(2,1)S(1)} %get-tuple-element.366), channel_id=1, source_target_pairs={{1,0},{2,1},{3,2},{4,3},{5,4},{6,5},{7,6},{9,8},{10,9},{11,10},{12... | collective-permute-start | bytes 46088 | tf_op jit(solution)/shard_map/while/body/eval_jaxpr/ppermute | solution.py:21
  243.3 8.0 %collective-permute-start.1 = (bf16[15,512]{1,0:T(8,128)(2,1)S(1)}, bf16[15,512]{1,0:T(8,128)(2,1)S(1)}, u32[]{:S(2)}, u32[]{:S(2)}) collective-permute-start(bf16[15,512]{1,0:T(8,128)(2,1)S(1)} %get-tuple-element.367), channel_id=1, source_target_pairs={{0,1},{1,2},{2,3},{3,4},{4,5},{5,6},{6,7},{8,9},{9,10},{10,11},{11... | collective-permute-start | bytes 46088 | tf_op jit(solution)/shard_map/while/body/eval_jaxpr/ppermute | solution.py:20
  256.8 12.3 %copy-start = (bf16[158,2688]{1,0:T(8,128)(2,1)}, bf16[158,2688]{1,0:T(8,128)(2,1)S(1)}, u32[]{:S(2)}) copy-start(bf16[158,2688]{1,0:T(8,128)(2,1)S(1)} %get-tuple-element.406) | copy-start | bytes 2548228 | tf_op jit(solution)/shard_map/while
  259.0 8.0 %collective-permute-start = (bf16[15,512]{1,0:T(8,128)(2,1)S(1)}, bf16[15,512]{1,0:T(8,128)(2,1)S(1)}, u32[]{:S(2)}, u32[]{:S(2)}) collective-permute-start(bf16[15,512]{1,0:T(8,128)(2,1)S(1)} %get-tuple-element.366), channel_id=1, source_target_pairs={{1,0},{2,1},{3,2},{4,3},{5,4},{6,5},{7,6},{9,8},{10,9},{11,10},{12... | collective-permute-start | bytes 46088 | tf_op jit(solution)/shard_map/while/body/eval_jaxpr/ppermute | solution.py:21
  260.9 8.0 %collective-permute-start.1 = (bf16[15,512]{1,0:T(8,128)(2,1)S(1)}, bf16[15,512]{1,0:T(8,128)(2,1)S(1)}, u32[]{:S(2)}, u32[]{:S(2)}) collective-permute-start(bf16[15,512]{1,0:T(8,128)(2,1)S(1)} %get-tuple-element.367), channel_id=1, source_target_pairs={{0,1},{1,2},{2,3},{3,4},{4,5},{5,6},{6,7},{8,9},{9,10},{10,11},{11... | collective-permute-start | bytes 46088 | tf_op jit(solution)/shard_map/while/body/eval_jaxpr/ppermute | solution.py:20
  274.4 14.9 %copy-start = (bf16[158,2688]{1,0:T(8,128)(2,1)}, bf16[158,2688]{1,0:T(8,128)(2,1)S(1)}, u32[]{:S(2)}) copy-start(bf16[158,2688]{1,0:T(8,128)(2,1)S(1)} %get-tuple-element.406) | copy-start | bytes 2548228 | tf_op jit(solution)/shard_map/while
  276.6 8.0 %collective-permute-start = (bf16[15,512]{1,0:T(8,128)(2,1)S(1)}, bf16[15,512]{1,0:T(8,128)(2,1)S(1)}, u32[]{:S(2)}, u32[]{:S(2)}) collective-permute-start(bf16[15,512]{1,0:T(8,128)(2,1)S(1)} %get-tuple-element.366), channel_id=1, source_target_pairs={{1,0},{2,1},{3,2},{4,3},{5,4},{6,5},{7,6},{9,8},{10,9},{11,10},{12... | collective-permute-start | bytes 46088 | tf_op jit(solution)/shard_map/while/body/eval_jaxpr/ppermute | solution.py:21
  281.1 8.0 %collective-permute-start.1 = (bf16[15,512]{1,0:T(8,128)(2,1)S(1)}, bf16[15,512]{1,0:T(8,128)(2,1)S(1)}, u32[]{:S(2)}, u32[]{:S(2)}) collective-permute-start(bf16[15,512]{1,0:T(8,128)(2,1)S(1)} %get-tuple-element.367), channel_id=1, source_target_pairs={{0,1},{1,2},{2,3},{3,4},{4,5},{5,6},{6,7},{8,9},{9,10},{10,11},{11... | collective-permute-start | bytes 46088 | tf_op jit(solution)/shard_map/while/body/eval_jaxpr/ppermute | solution.py:20
  294.5 12.3 %copy-start = (bf16[158,2688]{1,0:T(8,128)(2,1)}, bf16[158,2688]{1,0:T(8,128)(2,1)S(1)}, u32[]{:S(2)}) copy-start(bf16[158,2688]{1,0:T(8,128)(2,1)S(1)} %get-tuple-element.406) | copy-start | bytes 2548228 | tf_op jit(solution)/shard_map/while
  296.7 8.0 %collective-permute-start = (bf16[15,512]{1,0:T(8,128)(2,1)S(1)}, bf16[15,512]{1,0:T(8,128)(2,1)S(1)}, u32[]{:S(2)}, u32[]{:S(2)}) collective-permute-start(bf16[15,512]{1,0:T(8,128)(2,1)S(1)} %get-tuple-element.366), channel_id=1, source_target_pairs={{1,0},{2,1},{3,2},{4,3},{5,4},{6,5},{7,6},{9,8},{10,9},{11,10},{12... | collective-permute-start | bytes 46088 | tf_op jit(solution)/shard_map/while/body/eval_jaxpr/ppermute | solution.py:21
  298.6 8.0 %collective-permute-start.1 = (bf16[15,512]{1,0:T(8,128)(2,1)S(1)}, bf16[15,512]{1,0:T(8,128)(2,1)S(1)}, u32[]{:S(2)}, u32[]{:S(2)}) collective-permute-start(bf16[15,512]{1,0:T(8,128)(2,1)S(1)} %get-tuple-element.367), channel_id=1, source_target_pairs={{0,1},{1,2},{2,3},{3,4},{4,5},{5,6},{6,7},{8,9},{9,10},{10,11},{11... | collective-permute-start | bytes 46088 | tf_op jit(solution)/shard_map/while/body/eval_jaxpr/ppermute | solution.py:20
  (18 other events, 52.5 us)
where the time goes:
time: 316 us; the launch traced here: 314 us
  waiting for transfers between devices  179 us (57%)
  starting transfers between devices  71.5 us (23%)
  local copies, waits for them, and re-layouts  31.2 us (10%)
  matrix products  23.1 us (7%)
  other arithmetic  7.74 us (2%)
    all_to_all x1, waiting for transfers between devices, per_device(): lax.all_to_all(send_flux, 'patch', split_axis=1, concat_axis=1, tiled=True)  74.8 us
    all_to_all x1, waiting for transfers between devices, per_device(): lax.all_to_all(send_weight, 'patch', split_axis=1, concat_axis=1, tiled=T...  74.5 us
    ppermute x6, starting transfers between devices, extended(): before = lax.ppermute(last, axis, up)  24.2 us
    ppermute x6, waiting for transfers between devices, extended(): before = lax.ppermute(last, axis, up)  20.2 us
    ppermute x6, starting transfers between devices, extended(): after = lax.ppermute(leading, axis, down)  19.8 us
    all_to_all x1, starting transfers between devices, per_device(): lax.all_to_all(send_block, 'patch', split_axis=1, concat_axis=1, tiled=True)  17.1 us
    dot_general x6, matrix products, one_visit(): jnp.einsum('scbo,jb->jsco', smoothed, spatial_row, precision=lax.Precisio...  12.5 us
    dynamic_slice x12, local copies, waits for them, and re-layouts, per_device(): lax.map(one_visit, (flux_in, weight_in, block_in, spatial[0]))  10.7 us
  transfers between devices with their start and end apart: 15, of which 9 were waited for; matrix products, arithmetic and copies ran while one was open for 4% of the time, Pallas kernels for 0%

commit v1 on v0

v1 whole, which is shorter than its diff:
```python
import jax
import jax.numpy as jnp
import numpy as np
from jax import lax
from jax.experimental import pallas as pl
from jax.experimental.pallas import tpu as pltpu
from jax.sharding import PartitionSpec as P

MESH = pl.DeviceIdType.MESH
VISITS = 6
BASIS = 21
TAPS = 31
ROWS = 32
COLS = 512
ROUNDS = 3
PAIRS = (BASIS + 1) // 2
DEPTH = PAIRS * 128


def exchange_kernel(t_ref, k_ref, g_ref, h_ref, y, keys, z, s1, s1b, r1, sk, rk, s2, r2, sh, rh):
    n, bands = lax.axis_size("patch"), lax.axis_size("band")
    me, band = lax.axis_index("patch"), lax.axis_index("band")
    chips = n // 2
    chip, core = me // 2, me % 2

    barrier = pltpu.get_barrier_semaphore()

    def greet(d, carry):
        pl.semaphore_signal(
            barrier, inc=1, device_id={"patch": (me + d) % n}, device_id_type=MESH
        )
        return carry

    lax.fori_loop(1, n, greet, 0)

    @pl.when(band > 0)
    def _():
        pl.semaphore_signal(barrier, inc=1, device_id={"band": band - 1}, device_id_type=MESH)

    @pl.when(band < bands - 1)
    def _():
        pl.semaphore_signal(barrier, inc=1, device_id={"band": band + 1}, device_id_type=MESH)

    pl.semaphore_wait(
        barrier, n - 1 + (band + bands - 1) // bands + (2 * bands - 2 - band) // bands
    )

    def partner(i, count):
        half = (i + 1) // 2
        return count // 2 + half * (1 - 2 * (i % 2))

    def send_keys(i, carry):
        peer = (me + partner(i, n)) % n
        pltpu.make_async_remote_copy(
            k_ref.at[0], keys.at[me], sk, rk, device_id={"patch": peer}, device_id_type=MESH
        ).start()
        return carry

    lax.fori_loop(0, n - 1, send_keys, 0)
    pltpu.make_async_copy(k_ref.at[0], keys.at[me], rk).start()

    for q in range(ROUNDS):
        owner = q % 2

        def send_rows(i, carry):
            c = (chip + partner(i, chips)) % chips
            pltpu.make_async_remote_copy(
                t_ref.at[q * chips + c],
                y.at[q, me],
                s1.at[q],
                r1.at[q],
                device_id={"patch": 2 * c + owner},
                device_id_type=MESH,
            ).start()
            return carry

        lax.fori_loop(0, chips - 1, send_rows, 0)

        @pl.when(core == owner)
        def _():
            pltpu.make_async_copy(t_ref.at[q * chips + chip], y.at[q, me], r1.at[q]).start()

        @pl.when(core != owner)
        def _():
            pltpu.make_async_remote_copy(
                t_ref.at[q * chips + chip],
                y.at[q, me],
                s1b.at[q],
                r1.at[q],
                device_id={"patch": 2 * chip + owner},
                device_id_type=MESH,
            ).start()

    pltpu.make_async_copy(keys, keys, rk).wait()

    def relay(q):
        group = lax.broadcasted_iota(jnp.int32, (64, 128), 0) % 8
        lane_slot = lax.broadcasted_iota(jnp.int32, (64, 128), 1) // 16
        table = keys[:, 0, :]
        rows = []
        for visit in (2 * q, 2 * q + 1):
            picked = jnp.where((group + visit) % 8 == lane_slot, table, 0)
            picked = jnp.sum(picked.reshape(8, 8, 128), axis=1)
            rows.append(pltpu.roll(picked, (128 - 16 * visit) % 128, 1))
        second = jnp.broadcast_to(chip // (chips // 2), (8, 128))
        wanted = jnp.where(second == 0, rows[0], rows[1])
        pltpu.make_async_copy(y.at[q], y.at[q], r1.at[q]).wait()
        data = y[q].reshape(n * 16, 128)
        for part in range(4):
            place = lax.broadcasted_iota(jnp.int32, (256, 128), 0) + 256 * part
            chosen = jnp.concatenate(
                [
                    jnp.where(
                        jnp.broadcast_to(wanted[g : g + 1], (256, 128)) == place, 1.0, 0.0
                    ).astype(jnp.bfloat16)
                    for g in range(8)
                ],
                axis=1,
            )
            moved = jnp.dot(chosen, data, preferred_element_type=jnp.float32)
            z[q, part * 16 : (part + 1) * 16] = moved.reshape(16, 2, 8, 128).astype(jnp.bfloat16)

        def send_blocks(i, carry):
            peer = (me + partner(i, n)) % n
            pltpu.make_async_remote_copy(
                z.at[q, peer],
                g_ref.at[q * chips + chip],
                s2.at[q],
                r2.at[q],
                device_id={"patch": peer},
                device_id_type=MESH,
            ).start()
            return carry

        lax.fori_loop(0, n - 1, send_blocks, 0)
        pltpu.make_async_copy(z.at[q, me], g_ref.at[q * chips + chip], r2.at[q]).start()

    @pl.when(core == 0)
    def _():
        relay(0)
        relay(2)

    @pl.when(core == 1)
    def _():
        relay(1)

    def halo(visit, side):
        half, step = (1, 1) if side == 0 else (0, -1)
        return pltpu.make_async_remote_copy(
            g_ref.at[pl.ds(visit * 16, 8), half],
            h_ref.at[visit, side],
            sh.at[visit, side],
            rh.at[visit, side],
            device_id={"band": band + step},
            device_id_type=MESH,
        )

    for q in range(ROUNDS):
        part = g_ref.at[pl.ds(q * chips, chips)]
        pltpu.make_async_copy(part, part, r2.at[q]).wait()

        @pl.when(band < bands - 1)
        def _():
            halo(2 * q, 0).start()
            halo(2 * q + 1, 0).start()

        @pl.when(band > 0)
        def _():
            halo(2 * q, 1).start()
            halo(2 * q + 1, 1).start()

    @pl.when(band < bands - 1)
    def _():
        for visit in range(VISITS):
            halo(visit, 0).wait_send()
            halo(visit, 1).wait_recv()

    @pl.when(band > 0)
    def _():
        for visit in range(VISITS):
            halo(visit, 1).wait_send()
            halo(visit, 0).wait_recv()

    pltpu.make_async_copy(keys.at[pl.ds(0, n - 1)], keys.at[pl.ds(0, n - 1)], sk).wait()
    for q in range(ROUNDS):
        owner = q % 2
        sent = t_ref.at[pl.ds(0, chips - 1)]
        pltpu.make_async_copy(sent, sent, s1.at[q]).wait()

        @pl.when(core != owner)
        def _():
            pltpu.make_async_copy(t_ref.at[0], t_ref.at[0], s1b.at[q]).wait()

        @pl.when(core == owner)
        def _():
            relayed = z.at[q, pl.ds(0, n - 1)]
            pltpu.make_async_copy(relayed, relayed, s2.at[q]).wait()


def coadd_kernel(g_ref, h_ref, order_ref, worder_ref, cbase_ref, rbase_ref, coef_ref, o_ref,
                 ctable, rtable, filtered, num, den):
    band, bands = lax.axis_index("band"), lax.axis_size("band")
    row = lax.broadcasted_iota(jnp.int32, (128, 128), 0)
    lane = lax.broadcasted_iota(jnp.int32, (128, 128), 1)
    near = jnp.abs(row - lane) <= TAPS // 2
    for b in range(BASIS):
        taps = jnp.broadcast_to(cbase_ref[b : b + 1, :], (128, 128))
        cyclic = pltpu.roll(taps, 0, 1, stride=1, stride_axis=0)
        span = slice(b * 128, (b + 1) * 128)
        ctable[0:128, span] = jnp.where(near, cyclic, 0.0).astype(jnp.bfloat16)
        ctable[128:256, span] = jnp.where(near, 0.0, cyclic).astype(jnp.bfloat16)
    for pair in range(PAIRS):
        taps = jnp.broadcast_to(rbase_ref[pair : pair + 1, :], (ROWS, 128))
        rtable[:, pair * 128 : (pair + 1) * 128] = pltpu.roll(taps, 0, 1, stride=1, stride_axis=0)
    filtered[BASIS * 64 :, :] = jnp.zeros((DEPTH - BASIS * 64, COLS), jnp.bfloat16)
    num[...] = jnp.zeros_like(num)
    den[...] = jnp.zeros_like(den)
    first = (band * ROWS).astype(jnp.float32)
    rows_in = lax.broadcasted_iota(jnp.int32, (ROWS, 1), 0).astype(jnp.float32) + first
    u = (2.0 * rows_in + 1.0) / (bands * ROWS) - 1.0
    cols_in = lax.broadcasted_iota(jnp.int32, (1, COLS), 1).astype(jnp.float32)
    w = (2.0 * cols_in + 1.0) / COLS - 1.0
    above_on = jnp.broadcast_to(band, (8, 128)) > 0
    below_on = jnp.broadcast_to(band, (8, 128)) < bands - 1
    left_lane = lax.broadcasted_iota(jnp.int32, (256, 128), 1) < 64

    def one_visit(visit, carry):
        unit = visit * 16
        above = [jnp.where(above_on, h_ref[visit, 0, r].astype(jnp.float32), 0.0) for r in range(8)]
        below = [jnp.where(below_on, h_ref[visit, 1, r].astype(jnp.float32), 0.0) for r in range(8)]
        inner = [g_ref[unit + r, half].astype(jnp.float32) for r in range(8) for half in range(2)]
        rows = jnp.concatenate(above + inner + below, axis=0).astype(jnp.bfloat16)
        moved = jnp.dot(order_ref[...], rows, preferred_element_type=jnp.float32)
        beside = jnp.where(left_lane, moved[256:512], moved[512:768])
        window = jnp.concatenate([moved[0:256], beside], axis=1).astype(jnp.bfloat16)
        for b in range(BASIS):
            result = jnp.dot(
                window, ctable[:, b * 128 : (b + 1) * 128], preferred_element_type=jnp.float32
            ).astype(jnp.bfloat16)
            for c in range(4):
                filtered[b * 64 : (b + 1) * 64, c * 128 : (c + 1) * 128] = result[
                    c * 64 : (c + 1) * 64
                ]
        coef = coef_ref[visit]
        table = rtable[...]
        steady = table * (coef[0:1] + u * coef[1:2])
        slope = table * coef[2:3]
        exact = jnp.concatenate([steady, slope], axis=0)
        high = exact.astype(jnp.bfloat16)
        low = (exact - high.astype(jnp.float32)).astype(jnp.bfloat16)
        mixed = jnp.dot(
            jnp.concatenate([high, low], axis=0), filtered[...], preferred_element_type=jnp.float32
        )
        mixed = mixed[0:64] + mixed[64:128]
        matched = mixed[0:ROWS] + w * mixed[ROWS:64]
        weights = [g_ref[unit + 8 + r, half].astype(jnp.float32) for r in range(8) for half in range(2)]
        weights = jnp.concatenate(weights, axis=0).astype(jnp.bfloat16)
        weights = jnp.dot(worder_ref[...], weights, preferred_element_type=jnp.float32)
        weights = jnp.concatenate([weights[c * ROWS : (c + 1) * ROWS] for c in range(4)], axis=1)
        num[...] += weights * matched
        den[...] += weights
        return carry

    lax.fori_loop(0, VISITS, one_visit, 0)
    o_ref[...] = num[...] / den[...]


def orders():
    order = np.zeros((3, 4, 64, 256), np.float32)
    for c in range(4):
        for t in range(64):
            for kind, shift in ((0, 0), (1, 1), (2, -1)):
                d = c + shift
                if not 0 <= d < 4:
                    continue
                if t < 16:
                    place = (t % 8) * 8 + (t // 8) * 4 + d
                elif t < 48:
                    s = t - 16
                    place = 64 + (s % 8) * 16 + (s // 8) * 4 + d
                else:
                    s = t - 48
                    place = 192 + (s % 8) * 8 + (s // 8) * 4 + d
                order[kind, c, t, place] = 1.0
    worder = np.zeros((4, ROWS, 128), np.float32)
    for c in range(4):
        for s in range(ROWS):
            worder[c, s, (s % 8) * 16 + (s // 8) * 4 + c] = 1.0
    return order.reshape(768, 256), worder.reshape(128, 128)


def per_device(tile_flux, tile_weight, dest_patch, dest_block, basis, spatial):
    n = lax.axis_size("patch")
    chips = n // 2
    me = lax.axis_index("patch")
    units = jnp.stack([tile_flux, tile_weight], axis=1).transpose(0, 1, 3, 2, 4)
    units = units.reshape(VISITS * 16, 16, 128)
    key = dest_patch * 16 + dest_block
    slot = (jnp.arange(VISITS)[None, :, None] + me) % 8 == jnp.arange(8)[:, None, None]
    key_row = jnp.sum(jnp.where(slot, key[None], 0), axis=1).reshape(1, 1, 128)

    vmem = pl.BlockSpec(memory_space=pltpu.VMEM)
    dma = pltpu.SemaphoreType.DMA
    received, halo = pl.pallas_call(
        exchange_kernel,
        out_shape=(
            jax.ShapeDtypeStruct((VISITS * 16, 2, 8, 128), jnp.bfloat16),
            jax.ShapeDtypeStruct((VISITS, 2, 8, 8, 128), jnp.bfloat16),
        ),
        in_specs=[vmem, vmem],
        out_specs=(vmem, vmem),
        scratch_shapes=[
            pltpu.VMEM((ROUNDS, n, 16, 128), jnp.bfloat16),
            pltpu.VMEM((n, 1, 128), jnp.int32),
            pltpu.VMEM((ROUNDS, n, 2, 8, 128), jnp.bfloat16),
            dma((ROUNDS,)),
            dma((ROUNDS,)),
            dma((ROUNDS,)),
            dma,
            dma,
            dma((ROUNDS,)),
            dma((ROUNDS,)),
            dma((VISITS, 2)),
            dma((VISITS, 2)),
        ],
        compiler_params=pltpu.CompilerParams(collective_id=0, has_side_effects=True),
        name="exchange",
    )(units, key_row)

    order, worder = orders()
    ctaps = basis[0].astype(jnp.float32)
    cbase = jnp.concatenate(
        [ctaps[:, 15::-1], jnp.zeros((BASIS, 128 - TAPS), jnp.float32), ctaps[:, :15:-1]], axis=1
    )
    rtaps = jnp.pad(basis[1].astype(jnp.float32), ((0, 1), (1, 64 - TAPS - 1)))
    rbase = rtaps.reshape(PAIRS, 128)
    coef = jnp.pad(spatial[0], ((0, 0), (0, 0), (0, 1)))
    coef = jnp.broadcast_to(coef[..., None], coef.shape + (64,)).reshape(VISITS, 3, DEPTH)
    coadd = pl.pallas_call(
        coadd_kernel,
        out_shape=jax.ShapeDtypeStruct((ROWS, COLS), jnp.float32),
        in_specs=[vmem] * 7,
        out_specs=vmem,
        scratch_shapes=[
            pltpu.VMEM((256, BASIS * 128), jnp.bfloat16),
            pltpu.VMEM((ROWS, DEPTH), jnp.float32),
            pltpu.VMEM((DEPTH, COLS), jnp.bfloat16),
            pltpu.VMEM((ROWS, COLS), jnp.float32),
            pltpu.VMEM((ROWS, COLS), jnp.float32),
        ],
        name="coadd",
    )(
        received,
        halo,
        jnp.asarray(order, jnp.bfloat16),
        jnp.asarray(worder, jnp.bfloat16),
        cbase,
        rbase,
        coef,
    )
    return coadd[None]


def solution(mesh):
    in_specs = (
        P(None, ("patch", "band"), None, None),
        P(None, ("patch", "band"), None, None),
        P(None, ("patch", "band")),
        P(None, ("patch", "band")),
        P(),
        P("patch", None, None, None),
    )
    out_specs = P("patch", "band", None)
    return jax.shard_map(
        per_device, mesh=mesh, in_specs=in_specs, out_specs=out_specs, check_vma=False
    )
```

time: 316 us -> 78 us (0.25)
  waiting for transfers between devices: 179 us -> 0 us
  Pallas kernels: 0 us -> 72.3 us
  starting transfers between devices: 71.5 us -> 0 us
  local copies, waits for them, and re-layouts: 31.2 us -> 3.37 us
  matrix products: 23.1 us -> 0 us
  other arithmetic: 7.74 us -> 1.99 us
    all_to_all x3 -> x0, waiting for transfers between devices: 159 us -> none  [the longest x1 74.8 us: per_device(): lax.all_to_all(send_flux, 'patch', split_axis=1, concat_axis=1, tiled=True)]
    pallas_call x0 -> x2, Pallas kernels: none -> 72.3 us  [the longest x1 61 us: per_device(): pl.pallas_call(exchange_kernel, out_shape=(jax.ShapeDtypeStruct((VISITS *...]
    ppermute x12 -> x0, starting transfers between devices: 44.1 us -> none  [the longest x6 24.2 us: extended(): before = lax.ppermute(last, axis, up)]
    all_to_all x3 -> x0, starting transfers between devices: 27.5 us -> none  [the longest x1 17.1 us: per_device(): lax.all_to_all(send_block, 'patch', split_axis=1, concat_axis=1, tiled=True)]
    dot_general x34 -> x0, matrix products: 23.1 us -> none  [the longest x6 12.5 us: one_visit(): jnp.einsum('scbo,jb->jsco', smoothed, spatial_row, precision=lax.Precisio...]
    ppermute x12 -> x0, waiting for transfers between devices: 20.2 us -> none  [the longest x6 20.2 us: extended(): before = lax.ppermute(last, axis, up)]
    dynamic_slice x12 -> x0, local copies, waits for them, and re-layouts: 10.7 us -> none  [per_device(): lax.map(one_visit, (flux_in, weight_in, block_in, spatial[0]))]
    reshape x16 -> x3, local copies, waits for them, and re-layouts: 9.98 us -> 2.06 us  [the longest x1 0.8 us: per_device(): jnp.broadcast_to(coef[..., None], coef.shape + (64,))]
  transfers between devices with their start and end apart: 15 -> 0, of which waited for: 9 -> 0; matrix products, arithmetic and copies ran while one was open for 4% -> 0% of each run, Pallas kernels for 0% -> 0%
where the time goes in v1:
time: 78 us; the launch traced here: 77.8 us
  Pallas kernels  72.3 us (93%)
  local copies, waits for them, and re-layouts  3.37 us (4%)
  other arithmetic  1.99 us (3%)
    pallas_call x1, Pallas kernels, per_device(): pl.pallas_call(exchange_kernel, out_shape=(jax.ShapeDtypeStruct((VISITS *...  61 us
    pallas_call x1, Pallas kernels, per_device(): pl.pallas_call(coadd_kernel, out_shape=jax.ShapeDtypeStruct((ROWS, COLS),...  11.4 us

profile of v1, /device:TPU:6, one launch (start us, length us, event | category | flops | bytes accessed | tf_op | source)
XLA Modules:
  0.0 77.8 jit_solution(1908298909540230636)
XLA Ops:
  0.0 1.1 %maximum_bitcast_fusion = bf16[6,2,8,16,128]{4,2,3,0,1:T(8,128)(2,1)S(1)} fusion(bf16[6,1,16,8,128]{4,3,2,0,1:T(8,128)(2,1)} %bitcast.18, bf16[6,1,16,8,128]{4,3,2,0,1:T(8,128)(2,1)} %bitcast.19), kind=kLoop, calls=%fused_computation | loop fusion | flops 196608 | bytes 786432 | tf_op jit(solution)/shard_map/transpose | solution.py:296
  1.1 0.0 copy-start.2
  1.1 0.0 copy-start.3
  1.1 0.8 %copy.14 = bf16[6,2,8,16,128]{4,3,2,1,0:T(8,128)(2,1)} copy(bf16[6,2,8,16,128]{4,2,3,0,1:T(8,128)(2,1)S(1)} %maximum_bitcast_fusion) | data formatting | bytes 786432 | tf_op jit(solution)/shard_map/transpose | solution.py:296
  1.9 0.0 copy-done.2
  1.9 0.0 copy-done.3
  1.9 0.1 iota_compare_fusion
  2.0 0.1 select_reduce_fusion
  2.1 0.6 reshape.66.k_ref
  2.7 0.0 copy-start
  2.7 61.0 %exchange.1 = (bf16[96,2,8,128]{3,2,1,0:T(8,128)(2,1)}, bf16[6,2,8,8,128]{4,3,2,1,0:T(8,128)(2,1)}) custom-call(bf16[96,16,128]{2,1,0:T(8,128)(2,1)} %bitcast.17, s32[1,1,128]{2,1,0:T(1,128)} %reshape.66.k_ref), custom_call_target="tpu_custom_call" | custom-call | tf_op jit(solution)/shard_map/exchange/pallas_call | solution.py:304
  63.7 0.0 copy-done
  63.7 0.1 slice.17
  63.8 0.1 rev.7
  63.9 0.1 rev.6
  63.9 0.1 pad.12.clone
  64.0 0.7 pad_maximum_fusion.cbase_ref
  64.7 0.1 pad_convert_fusion
  64.8 0.0 copy-start.1
  64.8 0.7 reshape.72.rbase_ref
  65.4 0.0 copy-done.1
  65.5 0.1 broadcast_in_dim.39
  65.6 0.8 %reshape.69.coef_ref = f32[6,3,1408]{2,1,0:T(4,128)} reshape(f32[6,3,22,64]{3,2,1,0:T(8,128)S(1)} %broadcast_in_dim.39) | data formatting | bytes 202752 | tf_op jit(solution)/shard_map/reshape | solution.py:338
  66.4 11.4 %coadd.1 = f32[32,512]{1,0:T(8,128)} custom-call(bf16[96,2,8,128]{3,2,1,0:T(8,128)(2,1)} %get-tuple-element.7.g_ref, bf16[6,2,8,8,128]{4,3,2,1,0:T(8,128)(2,1)} %get-tuple-element.8.h_ref, bf16[768,256]{1,0:T(8,128)(2,1)} %constant.33.clone.order_ref, bf16[128,128]{1,0:T(8,128)(2,1)} %constant.34.clone.worder_ref, f32[21,128]{1,0:T(8,128)} %pad_maximum_fusion.cbase_ref, ...), custom_call_target="tpu_custom_call" | custom-call | tf_op jit(solution)/shard_map/coadd/pallas_call | solution.py:339
  (7 shorter events, 0.1 us)
Async XLA Ops:
  1.1 0.9 %copy-start.2 = (s32[6,16]{1,0:T(8,128)S(1)}, s32[6,16]{1,0:T(8,128)}, u32[]{:S(2)}) copy-start(s32[6,16]{1,0:T(8,128)} %param.11) | copy-start | bytes 1156
  1.1 0.8 %copy-start.3 = (s32[6,16]{1,0:T(8,128)S(1)}, s32[6,16]{1,0:T(8,128)}, u32[]{:S(2)}) copy-start(s32[6,16]{1,0:T(8,128)} %param.10) | copy-start | bytes 1156
  2.7 61.0 %copy-start = (bf16[2,21,31]{2,0,1:T(2,128)(2,1)S(1)}, bf16[2,21,31]{2,0,1:T(2,128)(2,1)}, u32[]{:S(2)}) copy-start(bf16[2,21,31]{2,0,1:T(2,128)(2,1)} %param.12) | copy-start | bytes 7816
  64.8 0.7 copy-start.1

commit v2 on v1

v2 whole, which is shorter than its diff:
```python
import jax
import jax.numpy as jnp
import numpy as np
from jax import lax
from jax.experimental import pallas as pl
from jax.experimental.pallas import tpu as pltpu
from jax.sharding import PartitionSpec as P

MESH = pl.DeviceIdType.MESH
VISITS = 6
BASIS = 21
TAPS = 31
ROWS = 32
COLS = 512
ROUNDS = 3
PAIRS = (BASIS + 1) // 2
DEPTH = PAIRS * 128
WIDE = PAIRS * 256


def bf16(value):
    return value.astype(jnp.bfloat16)


def iota(shape, dim):
    return lax.broadcasted_iota(jnp.int32, shape, dim)


def exact_dot(a, b):
    return jnp.dot(a, b, preferred_element_type=jnp.float32)


def one_hot(condition):
    return bf16(jnp.where(condition, 1.0, 0.0))


def kernel(flux_hbm, weight_hbm, patch_hbm, block_hbm, basis_hbm, spatial_hbm, order_hbm, worder_hbm,
           o_ref, tiles, dest, basis, spatial, both, order, worder, rows, key_row, y, keys, z, g, h,
           ctable, rtable, coefs, filtered, num, den,
           load, s1, s1b, r1, sk, rk, s2, r2, sh, rh):
    n, bands = lax.axis_size("patch"), lax.axis_size("band")
    me, band = lax.axis_index("patch"), lax.axis_index("band")
    chips = n // 2
    chip, core = me // 2, me % 2

    barrier = pltpu.get_barrier_semaphore()

    def greet(d, carry):
        pl.semaphore_signal(
            barrier, inc=1, device_id={"patch": (me + d) % n}, device_id_type=MESH
        )
        return carry

    lax.fori_loop(1, n, greet, 0)

    @pl.when(band > 0)
    def _():
        pl.semaphore_signal(barrier, inc=1, device_id={"band": band - 1}, device_id_type=MESH)

    @pl.when(band < bands - 1)
    def _():
        pl.semaphore_signal(barrier, inc=1, device_id={"band": band + 1}, device_id_type=MESH)

    loads = [
        pltpu.make_async_copy(source, target, load.at[i])
        for i, (source, target) in enumerate(
            (
                (patch_hbm, dest.at[0]),
                (block_hbm, dest.at[1]),
                (flux_hbm, tiles.at[0]),
                (weight_hbm, tiles.at[1]),
                (basis_hbm, basis),
                (spatial_hbm, spatial),
                (order_hbm, order),
                (worder_hbm, worder),
            )
        )
    ]
    for copy in loads:
        copy.start()

    loads[0].wait()
    loads[1].wait()
    spread = one_hot(iota((16, 128), 0) == iota((16, 128), 1) % 16)
    patch_lane = exact_dot(bf16(dest[0].astype(jnp.float32)), spread)
    block_lane = exact_dot(bf16(dest[1].astype(jnp.float32)), spread)
    mine = (iota((VISITS, 128), 0) + me) % 8 == iota((VISITS, 128), 1) // 16
    key_row[...] = jnp.sum(
        jnp.where(mine, patch_lane * 16.0 + block_lane, 0.0), axis=0, keepdims=True
    )
    turn = one_hot(
        (iota((128, 128), 0) % 16) * 8 + iota((128, 128), 0) // 16 == iota((128, 128), 1)
    )
    loads[2].wait()
    loads[3].wait()

    def turn_rows(visit, carry):
        for kind in range(2):
            pixels = bf16(
                jnp.concatenate(
                    [tiles[kind, visit, t].astype(jnp.float32) for t in range(16)], axis=0
                )
            )
            turned = bf16(exact_dot(turn, pixels))
            for r in range(8):
                rows[visit * 16 + kind * 8 + r] = turned[r * 16 : (r + 1) * 16]
        return carry

    lax.fori_loop(0, VISITS, turn_rows, 0)

    pl.semaphore_wait(
        barrier, n - 1 + (band + bands - 1) // bands + (2 * bands - 2 - band) // bands
    )

    def partner(i, count):
        half = (i + 1) // 2
        return count // 2 + half * (1 - 2 * (i % 2))

    def send_keys(i, carry):
        peer = (me + partner(i, n)) % n
        pltpu.make_async_remote_copy(
            key_row, keys.at[me], sk, rk, device_id={"patch": peer}, device_id_type=MESH
        ).start()
        return carry

    lax.fori_loop(0, n - 1, send_keys, 0)
    pltpu.make_async_copy(key_row, keys.at[me], rk).start()

    for q in range(ROUNDS):
        owner = q % 2

        def send_rows(i, carry):
            c = (chip + partner(i, chips)) % chips
            pltpu.make_async_remote_copy(
                rows.at[q * chips + c],
                y.at[q, me],
                s1.at[q],
                r1.at[q],
                device_id={"patch": 2 * c + owner},
                device_id_type=MESH,
            ).start()
            return carry

        lax.fori_loop(0, chips - 1, send_rows, 0)

        @pl.when(core == owner)
        def _():
            pltpu.make_async_copy(rows.at[q * chips + chip], y.at[q, me], r1.at[q]).start()

        @pl.when(core != owner)
        def _():
            pltpu.make_async_remote_copy(
                rows.at[q * chips + chip],
                y.at[q, me],
                s1b.at[q],
                r1.at[q],
                device_id={"patch": 2 * chip + owner},
                device_id_type=MESH,
            ).start()

    for copy in loads[4:]:
        copy.wait()
    tap, lane = iota((TAPS, 128), 0), iota((TAPS, 128), 1)
    for b in range(BASIS):
        both[2 * b : 2 * b + 2, 0:TAPS] = basis[b].astype(jnp.float32)
    taps_in = bf16(both[0 : 2 * BASIS, 0:TAPS])
    cbase = exact_dot(taps_in, one_hot((TAPS // 2 - tap + 128) % 128 == lane))
    rbase = [exact_dot(taps_in, one_hot(tap + 1 + 64 * odd == lane)) for odd in range(2)]
    near = jnp.abs(iota((128, 128), 0) - iota((128, 128), 1)) <= TAPS // 2
    for b in range(BASIS):
        taps = jnp.broadcast_to(cbase[2 * b : 2 * b + 1], (128, 128))
        cyclic = pltpu.roll(taps, 0, 1, stride=1, stride_axis=0)
        span = slice(b * 128, (b + 1) * 128)
        ctable[0:128, span] = bf16(jnp.where(near, cyclic, 0.0))
        ctable[128:256, span] = bf16(jnp.where(near, 0.0, cyclic))
    ctable[:, BASIS * 128 :] = jnp.zeros((256, WIDE - BASIS * 128), jnp.bfloat16)
    for pair in range(PAIRS):
        taps = rbase[0][4 * pair + 1 : 4 * pair + 2]
        if 2 * pair + 1 < BASIS:
            taps = taps + rbase[1][4 * pair + 3 : 4 * pair + 4]
        taps = jnp.broadcast_to(taps, (ROWS, 128))
        rtable[:, pair * 128 : (pair + 1) * 128] = pltpu.roll(taps, 0, 1, stride=1, stride_axis=0)
    widen = one_hot(iota((BASIS, DEPTH), 0) == iota((BASIS, DEPTH), 1) // 64)
    for visit in range(VISITS):
        for term in range(3):
            coefs[visit * 8 + term : visit * 8 + term + 1, 0:BASIS] = spatial[visit, term]
    plain = coefs[:, 0:BASIS]
    plain = jnp.where(iota(plain.shape, 0) % 8 < 3, plain, 0.0)
    top = bf16(plain)
    rest = plain - top.astype(jnp.float32)
    middle = bf16(rest)
    bottom = bf16(rest - middle.astype(jnp.float32))
    coefs[...] = exact_dot(top, widen) + exact_dot(middle, widen) + exact_dot(bottom, widen)
    num[...] = jnp.zeros_like(num)
    den[...] = jnp.zeros_like(den)

    pltpu.make_async_copy(keys, keys, rk).wait()

    def relay(q):
        group = iota((64, 128), 0) % 8
        lane_slot = iota((64, 128), 1) // 16
        table = keys[:, 0, :]
        options = []
        for visit in (2 * q, 2 * q + 1):
            picked = jnp.where((group + visit) % 8 == lane_slot, table, 0.0)
            picked = jnp.sum(picked.reshape(8, 8, 128), axis=1)
            options.append(pltpu.roll(picked, (128 - 16 * visit) % 128, 1))
        second = jnp.broadcast_to(chip // (chips // 2), (8, 128))
        wanted = jnp.where(second == 0, options[0], options[1]).astype(jnp.int32)
        pltpu.make_async_copy(y.at[q], y.at[q], r1.at[q]).wait()
        data = y[q].reshape(n * 16, 128)
        for part in range(4):
            place = iota((256, 128), 0) + 256 * part
            chosen = jnp.concatenate(
                [
                    one_hot(jnp.broadcast_to(wanted[k : k + 1], (256, 128)) == place)
                    for k in range(8)
                ],
                axis=1,
            )
            moved = exact_dot(chosen, data)
            z[q, part * 16 : (part + 1) * 16] = bf16(moved.reshape(16, 2, 8, 128))

        def send_blocks(i, carry):
            peer = (me + partner(i, n)) % n
            pltpu.make_async_remote_copy(
                z.at[q, peer],
                g.at[q * chips + chip],
                s2.at[q],
                r2.at[q],
                device_id={"patch": peer},
                device_id_type=MESH,
            ).start()
            return carry

        lax.fori_loop(0, n - 1, send_blocks, 0)
        pltpu.make_async_copy(z.at[q, me], g.at[q * chips + chip], r2.at[q]).start()

    @pl.when(core == 0)
    def _():
        relay(0)
        relay(2)

    @pl.when(core == 1)
    def _():
        relay(1)

    def halo(visit, side):
        half, step = (1, 1) if side == 0 else (0, -1)
        return pltpu.make_async_remote_copy(
            g.at[pl.ds(visit * 16, 8), half],
            h.at[visit, side],
            sh.at[visit, side],
            rh.at[visit, side],
            device_id={"band": band + step},
            device_id_type=MESH,
        )

    first = (band * ROWS).astype(jnp.float32)
    u = (2.0 * (iota((ROWS, 1), 0).astype(jnp.float32) + first) + 1.0) / (bands * ROWS) - 1.0
    w = (2.0 * iota((1, COLS), 1).astype(jnp.float32) + 1.0) / COLS - 1.0
    above_on = jnp.broadcast_to(band, (8, 128)) > 0
    below_on = jnp.broadcast_to(band, (8, 128)) < bands - 1
    left_lane = iota((256, 128), 1) < 64

    def one_visit(visit, carry):
        unit = visit * 16
        above = [jnp.where(above_on, h[visit, 0, r].astype(jnp.float32), 0.0) for r in range(8)]
        below = [jnp.where(below_on, h[visit, 1, r].astype(jnp.float32), 0.0) for r in range(8)]
        inner = [g[unit + r, half].astype(jnp.float32) for r in range(8) for half in range(2)]
        image = bf16(jnp.concatenate(above + inner + below, axis=0))
        moved = exact_dot(order[...], image)
        beside = jnp.where(left_lane, moved[256:512], moved[512:768])
        window = bf16(jnp.concatenate([moved[0:256], beside], axis=1))
        for pair in range(PAIRS):
            result = bf16(exact_dot(window, ctable[:, pair * 256 : (pair + 1) * 256]))
            for odd in range(2):
                b = 2 * pair + odd
                for c in range(4):
                    filtered[b * 64 : (b + 1) * 64, c * 128 : (c + 1) * 128] = result[
                        c * 64 : (c + 1) * 64, odd * 128 : (odd + 1) * 128
                    ]
        coef = coefs[pl.ds(pl.multiple_of(visit * 8, 8), 8)]
        table = rtable[...]
        steady = table * (coef[0:1] + u * coef[1:2])
        slope = table * coef[2:3]
        full = jnp.concatenate([steady, slope], axis=0)
        high = bf16(full)
        low = bf16(full - high.astype(jnp.float32))
        mixed = exact_dot(jnp.concatenate([high, low], axis=0), filtered[...])
        mixed = mixed[0:64] + mixed[64:128]
        matched = mixed[0:ROWS] + w * mixed[ROWS:64]
        weights = [g[unit + 8 + r, half].astype(jnp.float32) for r in range(8) for half in range(2)]
        weights = exact_dot(worder[...], bf16(jnp.concatenate(weights, axis=0)))
        weights = jnp.concatenate([weights[c * ROWS : (c + 1) * ROWS] for c in range(4)], axis=1)
        num[...] += weights * matched
        den[...] += weights
        return carry

    def share_edges(q):
        part = g.at[pl.ds(q * chips, chips)]
        pltpu.make_async_copy(part, part, r2.at[q]).wait()

        @pl.when(band < bands - 1)
        def _():
            halo(2 * q, 0).start()
            halo(2 * q + 1, 0).start()

        @pl.when(band > 0)
        def _():
            halo(2 * q, 1).start()
            halo(2 * q + 1, 1).start()

    def wait_edges(q):
        @pl.when(band < bands - 1)
        def _():
            halo(2 * q, 1).wait_recv()
            halo(2 * q + 1, 1).wait_recv()

        @pl.when(band > 0)
        def _():
            halo(2 * q, 0).wait_recv()
            halo(2 * q + 1, 0).wait_recv()

    share_edges(0)
    share_edges(1)
    wait_edges(0)
    wait_edges(1)
    lax.fori_loop(0, 3, one_visit, 0)
    share_edges(2)
    lax.fori_loop(3, 4, one_visit, 0)
    wait_edges(2)
    lax.fori_loop(4, 6, one_visit, 0)
    o_ref[...] = num[...] / den[...]

    @pl.when(band < bands - 1)
    def _():
        for visit in range(VISITS):
            halo(visit, 0).wait_send()

    @pl.when(band > 0)
    def _():
        for visit in range(VISITS):
            halo(visit, 1).wait_send()

    pltpu.make_async_copy(keys.at[pl.ds(0, n - 1)], keys.at[pl.ds(0, n - 1)], sk).wait()
    for q in range(ROUNDS):
        owner = q % 2
        sent = rows.at[pl.ds(0, chips - 1)]
        pltpu.make_async_copy(sent, sent, s1.at[q]).wait()

        @pl.when(core != owner)
        def _():
            pltpu.make_async_copy(rows.at[0], rows.at[0], s1b.at[q]).wait()

        @pl.when(core == owner)
        def _():
            relayed = z.at[q, pl.ds(0, n - 1)]
            pltpu.make_async_copy(relayed, relayed, s2.at[q]).wait()


def orders():
    order = np.zeros((3, 4, 64, 256), np.float32)
    for c in range(4):
        for t in range(64):
            for kind, shift in ((0, 0), (1, 1), (2, -1)):
                d = c + shift
                if not 0 <= d < 4:
                    continue
                if t < 16:
                    place = (t % 8) * 8 + (t // 8) * 4 + d
                elif t < 48:
                    s = t - 16
                    place = 64 + (s % 8) * 16 + (s // 8) * 4 + d
                else:
                    s = t - 48
                    place = 192 + (s % 8) * 8 + (s // 8) * 4 + d
                order[kind, c, t, place] = 1.0
    worder = np.zeros((4, ROWS, 128), np.float32)
    for c in range(4):
        for s in range(ROWS):
            worder[c, s, (s % 8) * 16 + (s // 8) * 4 + c] = 1.0
    return order.reshape(768, 256), worder.reshape(128, 128)


def per_device(tile_flux, tile_weight, dest_patch, dest_block, basis, spatial):
    n = lax.axis_size("patch")
    vmem, dma = pltpu.VMEM, pltpu.SemaphoreType.DMA
    order, worder = orders()
    coadd = pl.pallas_call(
        kernel,
        out_shape=jax.ShapeDtypeStruct((ROWS, COLS), jnp.float32),
        in_specs=[pl.BlockSpec(memory_space=pl.ANY)] * 8,
        out_specs=pl.BlockSpec(memory_space=vmem),
        scratch_shapes=[
            vmem((2, VISITS, 16, 8, 128), jnp.bfloat16),
            vmem((2, VISITS, 16), jnp.int32),
            vmem((BASIS, 2, TAPS), jnp.bfloat16),
            vmem((VISITS, 3, 1, BASIS), jnp.float32),
            vmem((48, 128), jnp.float32),
            vmem((768, 256), jnp.bfloat16),
            vmem((128, 128), jnp.bfloat16),
            vmem((VISITS * 16, 16, 128), jnp.bfloat16),
            vmem((1, 128), jnp.float32),
            vmem((ROUNDS, n, 16, 128), jnp.bfloat16),
            vmem((n, 1, 128), jnp.float32),
            vmem((ROUNDS, n, 2, 8, 128), jnp.bfloat16),
            vmem((VISITS * 16, 2, 8, 128), jnp.bfloat16),
            vmem((VISITS, 2, 8, 8, 128), jnp.bfloat16),
            vmem((256, WIDE), jnp.bfloat16),
            vmem((ROWS, DEPTH), jnp.float32),
            vmem((VISITS * 8, DEPTH), jnp.float32),
            vmem((DEPTH, COLS), jnp.bfloat16),
            vmem((ROWS, COLS), jnp.float32),
            vmem((ROWS, COLS), jnp.float32),
            dma((8,)),
            dma((ROUNDS,)),
            dma((ROUNDS,)),
            dma((ROUNDS,)),
            dma,
            dma,
            dma((ROUNDS,)),
            dma((ROUNDS,)),
            dma((VISITS, 2)),
            dma((VISITS, 2)),
        ],
        compiler_params=pltpu.CompilerParams(collective_id=0, has_side_effects=True),
        name="coadd",
    )(
        tile_flux,
        tile_weight,
        dest_patch,
        dest_block,
        basis.transpose(1, 0, 2),
        spatial.transpose(1, 2, 0, 3),
        jnp.asarray(order, jnp.bfloat16),
        jnp.asarray(worder, jnp.bfloat16),
    )
    return coadd[None]


def solution(mesh):
    in_specs = (
        P(None, ("patch", "band"), None, None),
        P(None, ("patch", "band"), None, None),
        P(None, ("patch", "band")),
        P(None, ("patch", "band")),
        P(),
        P("patch", None, None, None),
    )
    out_specs = P("patch", "band", None)
    return jax.shard_map(
        per_device, mesh=mesh, in_specs=in_specs, out_specs=out_specs, check_vma=False
    )
```

time: 78 us -> 67.9 us (0.87); the launches traced: 77.8 us -> 66.7 us
  Pallas kernels: 72.3 us -> 65.3 us
  other arithmetic: 1.99 us -> 0 us
  local copies, waits for them, and re-layouts: 3.37 us -> 1.47 us
    pallas_call x2 -> x1, Pallas kernels: 72.3 us -> 65.3 us  [per_device(): pl.pallas_call(kernel, out_shape=jax.ShapeDtypeStruct((ROWS, COLS), jnp.f...]
    reshape x3 -> x0, local copies, waits for them, and re-layouts: 2.06 us -> none  [the longest x1 0.8 us: per_device(): jnp.broadcast_to(coef[..., None], coef.shape + (64,))]
    unnamed x9 -> x1, local copies, waits for them, and re-layouts: 0.05 us -> 1.47 us
    transpose x1 -> x0, other arithmetic: 1.06 us -> none  [per_device(): units = jnp.stack([tile_flux, tile_weight], axis=1).transpose(0, 1, 3, 2, 4)]
    transpose x1 -> x0, local copies, waits for them, and re-layouts: 0.82 us -> none  [per_device(): units = jnp.stack([tile_flux, tile_weight], axis=1).transpose(0, 1, 3, 2, 4)]
where the time goes in v2:
time: 67.9 us; the launch traced here: 66.7 us
  Pallas kernels  65.3 us (96%)
  local copies, waits for them, and re-layouts  1.47 us (2%)
    pallas_call x1, Pallas kernels, per_device(): pl.pallas_call(kernel, out_shape=jax.ShapeDtypeStruct((ROWS, COLS), jnp.f...  65.3 us
    unnamed x1, local copies, waits for them, and re-layouts  1.47 us

profile of v2, /device:TPU:6, one launch (start us, length us, event | category | flops | bytes accessed | tf_op | source)
XLA Modules:
  0.0 66.7 jit_solution(1478674243459883727)
XLA Ops:
  0.0 65.3 %coadd.1 = f32[32,512]{1,0:T(8,128)} custom-call(bf16[6,16,8,128]{3,2,1,0:T(8,128)(2,1)} %flux_hbm.1, bf16[6,16,8,128]{3,2,1,0:T(8,128)(2,1)} %weight_hbm.1, s32[6,16]{1,0:T(8,128)} %patch_hbm.1, s32[6,16]{1,0:T(8,128)} %block_hbm.1, bf16[21,2,31]{2,1,0:T(2,128)(2,1)} %bitcast.4, f32[6,3,1,21]{3,2,1,0:T(1,128)} %bitcast.5, ...), custom_call_target="tpu_custom_call" | custom-call | tf_op jit(solution)/shard_map/coadd/pallas_call | solution.py:390
  65.3 1.5 %copy.10 = f32[1,32,512]{2,1,0:T(8,128)} copy(f32[1,32,512]{2,1,0:T(8,128)} %bitcast.3) | data formatting | bytes 131072

commit v3 on v2

--- a/solution.py
+++ b/solution.py
@@ -12,7 +12,10 @@
 TAPS = 31
 ROWS = 32
 COLS = 512
-ROUNDS = 3
+NEAR = 4
+AHEAD = 3
+ROUNDS = 6
+LEVELS = ((4, 0), (0, ROUNDS))
 PAIRS = (BASIS + 1) // 2
 DEPTH = PAIRS * 128
 WIDE = PAIRS * 256
@@ -36,22 +39,30 @@
 
 def kernel(flux_hbm, weight_hbm, patch_hbm, block_hbm, basis_hbm, spatial_hbm, order_hbm, worder_hbm,
            o_ref, tiles, dest, basis, spatial, both, order, worder, rows, key_row, y, keys, z, g, h,
-           ctable, rtable, coefs, filtered, num, den,
-           load, s1, s1b, r1, sk, rk, s2, r2, sh, rh):
+           ctable, rtable, coefs, filtered, matched, num, den,
+           load, heard, s1, s1b, r1, sk, rk, sk4, rk4, s2, r2, sh, rh):
     n, bands = lax.axis_size("patch"), lax.axis_size("band")
     me, band = lax.axis_index("patch"), lax.axis_index("band")
-    chips = n // 2
-    chip, core = me // 2, me % 2
+    core = me % 2
+
+    zs = n // 4
+    height, lane4 = me // 4, me % 4
+
+    def peer_at(step, place):
+        return ((height + step + zs) % zs) * 4 + place
 
     barrier = pltpu.get_barrier_semaphore()
 
-    def greet(d, carry):
-        pl.semaphore_signal(
-            barrier, inc=1, device_id={"patch": (me + d) % n}, device_id_type=MESH
-        )
+    def greet(i, carry):
+        peer = peer_at(i // 4 - NEAR, i % 4)
+        pl.semaphore_signal(barrier, inc=1, device_id={"patch": peer}, device_id_type=MESH)
         return carry
 
-    lax.fori_loop(1, n, greet, 0)
+    lax.fori_loop(0, NEAR * 4, greet, 0)
+    lax.fori_loop(NEAR * 4 + 4, NEAR * 8 + 4, greet, 0)
+    for d in range(1, 4):
+        peer = peer_at(0, (lane4 + d) % 4)
+        pl.semaphore_signal(barrier, inc=1, device_id={"patch": peer}, device_id_type=MESH)
 
     @pl.when(band > 0)
     def _():
@@ -84,10 +95,9 @@
     spread = one_hot(iota((16, 128), 0) == iota((16, 128), 1) % 16)
     patch_lane = exact_dot(bf16(dest[0].astype(jnp.float32)), spread)
     block_lane = exact_dot(bf16(dest[1].astype(jnp.float32)), spread)
-    mine = (iota((VISITS, 128), 0) + me) % 8 == iota((VISITS, 128), 1) // 16
-    key_row[...] = jnp.sum(
-        jnp.where(mine, patch_lane * 16.0 + block_lane, 0.0), axis=0, keepdims=True
-    )
+    key_lane = patch_lane * 16.0 + block_lane
+    key_lane = jnp.where(iota((VISITS, 128), 0) == iota((VISITS, 128), 1) // 16, key_lane, 0.0)
+    key_row[...] = jnp.sum(key_lane, axis=0, keepdims=True)
     turn = one_hot(
         (iota((128, 128), 0) % 16) * 8 + iota((128, 128), 0) // 16 == iota((128, 128), 1)
     )
@@ -103,60 +113,116 @@
             )
             turned = bf16(exact_dot(turn, pixels))
             for r in range(8):
-                rows[visit * 16 + kind * 8 + r] = turned[r * 16 : (r + 1) * 16]
+                rows[kind * VISITS * 8 + visit * 8 + r] = turned[r * 16 : (r + 1) * 16]
         return carry
 
     lax.fori_loop(0, VISITS, turn_rows, 0)
 
     pl.semaphore_wait(
-        barrier, n - 1 + (band + bands - 1) // bands + (2 * bands - 2 - band) // bands
+        barrier, NEAR * 8 + 3 + (band + bands - 1) // bands + (2 * bands - 2 - band) // bands
     )
 
-    def partner(i, count):
-        half = (i + 1) // 2
-        return count // 2 + half * (1 - 2 * (i % 2))
-
-    def send_keys(i, carry):
-        peer = (me + partner(i, n)) % n
+    def send_key(step):
         pltpu.make_async_remote_copy(
-            key_row, keys.at[me], sk, rk, device_id={"patch": peer}, device_id_type=MESH
+            key_row,
+            keys.at[lane4, height],
+            sk,
+            rk,
+            device_id={"patch": peer_at(step, lane4)},
+            device_id_type=MESH,
         ).start()
-        return carry
-
-    lax.fori_loop(0, n - 1, send_keys, 0)
-    pltpu.make_async_copy(key_row, keys.at[me], rk).start()
-
-    for q in range(ROUNDS):
-        owner = q % 2
-
-        def send_rows(i, carry):
-            c = (chip + partner(i, chips)) % chips
-            pltpu.make_async_remote_copy(
-                rows.at[q * chips + c],
-                y.at[q, me],
-                s1.at[q],
-                r1.at[q],
-                device_id={"patch": 2 * c + owner},
-                device_id_type=MESH,
-            ).start()
+
+    def send_row(turn_no, step):
+        place = (turn_no % 2) * 2 + (turn_no // 2) % 2
+        pltpu.make_async_remote_copy(
+            rows.at[turn_no * 16 + (height + step + zs) % zs],
+            y.at[turn_no // 4, me],
+            s1.at[turn_no],
+            r1.at[turn_no // 4],
+            device_id={"patch": peer_at(step, place)},
+            device_id_type=MESH,
+        ).start()
+
+    def send_ring(inner, outer, rounds, with_keys):
+        def one(i, carry):
+            reach = outer - i
+            for step in (reach, -reach):
+                if with_keys:
+                    send_key(step)
+                for turn_no in rounds:
+                    send_row(turn_no, step)
             return carry
 
-        lax.fori_loop(0, chips - 1, send_rows, 0)
-
-        @pl.when(core == owner)
-        def _():
-            pltpu.make_async_copy(rows.at[q * chips + chip], y.at[q, me], r1.at[q]).start()
-
-        @pl.when(core != owner)
-        def _():
-            pltpu.make_async_remote_copy(
-                rows.at[q * chips + chip],
-                y.at[q, me],
-                s1b.at[q],
-                r1.at[q],
-                device_id={"patch": 2 * chip + owner},
-                device_id_type=MESH,
-            ).start()
+        lax.fori_loop(0, outer - inner, one, 0)
+        if outer == zs // 2 - 1:
+            if with_keys:
+                send_key(zs // 2)
+            for turn_no in rounds:
+                send_row(turn_no, zs // 2)
+
+    pltpu.make_async_copy(key_row, keys.at[lane4, height], rk).start()
+
+    def own_height(rounds):
+        for turn_no in rounds:
+            place = (turn_no % 2) * 2 + (turn_no // 2) % 2
+
+            @pl.when(lane4 == place)
+            def _():
+                pltpu.make_async_copy(
+                    rows.at[turn_no * 16 + height], y.at[turn_no // 4, me], r1.at[turn_no // 4]
+                ).start()
+
+            @pl.when(lane4 != place)
+            def _():
+                pltpu.make_async_remote_copy(
+                    rows.at[turn_no * 16 + height],
+                    y.at[turn_no // 4, me],
+                    s1b.at[turn_no],
+                    r1.at[turn_no // 4],
+                    device_id={"patch": peer_at(0, place)},
+                    device_id_type=MESH,
+                ).start()
+
+    known, sent = NEAR, [0] * ROUNDS
+    for level, (reach, count) in enumerate(LEVELS):
+        if reach:
+            for step in (reach, -reach):
+                pl.semaphore_signal(
+                    heard.at[level],
+                    inc=1,
+                    device_id={"patch": peer_at(step, lane4)},
+                    device_id_type=MESH,
+                )
+        if level == 0:
+            send_ring(0, known, (0,), True)
+            if AHEAD > 1:
+                send_ring(0, known, tuple(range(1, AHEAD)), False)
+            own_height(range(ROUNDS))
+            sent = [known] * AHEAD + [0] * (ROUNDS - AHEAD)
+        else:
+            for turn_no in range(count):
+                send_ring(sent[turn_no], known, (turn_no,), sent[turn_no] == before and turn_no == 0)
+                sent[turn_no] = known
+        before = known
+        if reach:
+            pl.semaphore_wait(heard.at[level], 2)
+            known = min(known + reach, zs // 2 - 1)
+
+    column = keys.at[lane4]
+    pltpu.make_async_copy(column, column, rk).wait()
+
+    def forward(d):
+        return pltpu.make_async_remote_copy(
+            column,
+            keys.at[lane4],
+            sk4.at[d - 1],
+            rk4.at[d - 1],
+            device_id={"patch": peer_at(0, (lane4 + d) % 4)},
+            device_id_type=MESH,
+        )
+
+    for d in range(1, 4):
+        forward(d).start()
 
     for copy in loads[4:]:
         copy.wait()
@@ -194,21 +260,29 @@
     num[...] = jnp.zeros_like(num)
     den[...] = jnp.zeros_like(den)
 
-    pltpu.make_async_copy(keys, keys, rk).wait()
-
-    def relay(q):
-        group = iota((64, 128), 0) % 8
-        lane_slot = iota((64, 128), 1) // 16
-        table = keys[:, 0, :]
-        options = []
-        for visit in (2 * q, 2 * q + 1):
-            picked = jnp.where((group + visit) % 8 == lane_slot, table, 0.0)
-            picked = jnp.sum(picked.reshape(8, 8, 128), axis=1)
-            options.append(pltpu.roll(picked, (128 - 16 * visit) % 128, 1))
-        second = jnp.broadcast_to(chip // (chips // 2), (8, 128))
-        wanted = jnp.where(second == 0, options[0], options[1]).astype(jnp.int32)
-        pltpu.make_async_copy(y.at[q], y.at[q], r1.at[q]).wait()
-        data = y[q].reshape(n * 16, 128)
+    for d in range(1, 4):
+        forward(d).wait_recv()
+
+    def partner(i):
+        half = (i + 1) // 2
+        return n // 2 + half * (1 - 2 * (i % 2))
+
+    def relay(slot):
+        turn_no = me // 2 % 2 + 2 * core if slot == 0 else me // 2 % 2 + 4
+        visit = 2 * (turn_no % 3) + height // 8
+        table = keys[...].reshape(64, 128)
+        patch_of = jnp.floor(table * (1.0 / 16.0))
+        block_of = table - 16.0 * patch_of
+        spread = one_hot(iota((128, 128), 0) == iota((128, 128), 1) % 16 + 16 * visit)
+        source = iota((64, 128), 0) % 16 % 2 * 4 + iota((64, 128), 0) // 16
+        held = source == iota((64, 128), 1) // 16
+        gather = one_hot(iota((8, 64), 1) % 16 // 2 == iota((8, 64), 0))
+        patch_of = jnp.where(held, exact_dot(bf16(patch_of), spread), 0.0)
+        block_of = jnp.where(held, exact_dot(bf16(block_of), spread), 0.0)
+        wanted = exact_dot(gather, bf16(patch_of)) * 16.0 + exact_dot(gather, bf16(block_of))
+        wanted = wanted.astype(jnp.int32)
+        pltpu.make_async_copy(y.at[slot], y.at[slot], r1.at[slot]).wait()
+        data = y[slot].reshape(n * 16, 128)
         for part in range(4):
             place = iota((256, 128), 0) + 256 * part
             chosen = jnp.concatenate(
@@ -219,36 +293,33 @@
                 axis=1,
             )
             moved = exact_dot(chosen, data)
-            z[q, part * 16 : (part + 1) * 16] = bf16(moved.reshape(16, 2, 8, 128))
+            z[slot, part * 16 : (part + 1) * 16] = bf16(moved.reshape(16, 2, 8, 128))
 
         def send_blocks(i, carry):
-            peer = (me + partner(i, n)) % n
+            peer = (me + partner(i)) % n
             pltpu.make_async_remote_copy(
-                z.at[q, peer],
-                g.at[q * chips + chip],
-                s2.at[q],
-                r2.at[q],
+                z.at[slot, peer],
+                g.at[turn_no * 16 + height],
+                s2.at[slot],
+                r2.at[turn_no],
                 device_id={"patch": peer},
                 device_id_type=MESH,
             ).start()
             return carry
 
         lax.fori_loop(0, n - 1, send_blocks, 0)
-        pltpu.make_async_copy(z.at[q, me], g.at[q * chips + chip], r2.at[q]).start()
+        pltpu.make_async_copy(z.at[slot, me], g.at[turn_no * 16 + height], r2.at[turn_no]).start()
+
+    relay(0)
 
     @pl.when(core == 0)
-    def _():
-        relay(0)
-        relay(2)
-
-    @pl.when(core == 1)
     def _():
         relay(1)
 
     def halo(visit, side):
         half, step = (1, 1) if side == 0 else (0, -1)
         return pltpu.make_async_remote_copy(
-            g.at[pl.ds(visit * 16, 8), half],
+            g.at[pl.ds(visit * 8, 8), half],
             h.at[visit, side],
             sh.at[visit, side],
             rh.at[visit, side],
@@ -264,7 +335,7 @@
     left_lane = iota((256, 128), 1) < 64
 
     def one_visit(visit, carry):
-        unit = visit * 16
+        unit = visit * 8
         above = [jnp.where(above_on, h[visit, 0, r].astype(jnp.float32), 0.0) for r in range(8)]
         below = [jnp.where(below_on, h[visit, 1, r].astype(jnp.float32), 0.0) for r in range(8)]
         inner = [g[unit + r, half].astype(jnp.float32) for r in range(8) for half in range(2)]
@@ -289,48 +360,59 @@
         low = bf16(full - high.astype(jnp.float32))
         mixed = exact_dot(jnp.concatenate([high, low], axis=0), filtered[...])
         mixed = mixed[0:64] + mixed[64:128]
-        matched = mixed[0:ROWS] + w * mixed[ROWS:64]
-        weights = [g[unit + 8 + r, half].astype(jnp.float32) for r in range(8) for half in range(2)]
+        matched[visit] = mixed[0:ROWS] + w * mixed[ROWS:64]
+        return carry
+
+    def weigh(visit, carry):
+        unit = (VISITS + visit) * 8
+        weights = [g[unit + r, half].astype(jnp.float32) for r in range(8) for half in range(2)]
         weights = exact_dot(worder[...], bf16(jnp.concatenate(weights, axis=0)))
         weights = jnp.concatenate([weights[c * ROWS : (c + 1) * ROWS] for c in range(4)], axis=1)
-        num[...] += weights * matched
+        num[...] += weights * matched[visit]
         den[...] += weights
         return carry
 
-    def share_edges(q):
-        part = g.at[pl.ds(q * chips, chips)]
-        pltpu.make_async_copy(part, part, r2.at[q]).wait()
+    def arrived(turn_no):
+        part = g.at[pl.ds(turn_no * 16, 16)]
+        pltpu.make_async_copy(part, part, r2.at[turn_no]).wait()
+
+    def share_edges(turn_no):
+        arrived(turn_no)
 
         @pl.when(band < bands - 1)
         def _():
-            halo(2 * q, 0).start()
-            halo(2 * q + 1, 0).start()
+            halo(2 * turn_no, 0).start()
+            halo(2 * turn_no + 1, 0).start()
 
         @pl.when(band > 0)
         def _():
-            halo(2 * q, 1).start()
-            halo(2 * q + 1, 1).start()
-
-    def wait_edges(q):
+            halo(2 * turn_no, 1).start()
+            halo(2 * turn_no + 1, 1).start()
+
+    def filter_pair(turn_no, carry):
+        @pl.when(turn_no < 2)
+        def _():
+            share_edges(turn_no + 1)
+
         @pl.when(band < bands - 1)
         def _():
-            halo(2 * q, 1).wait_recv()
-            halo(2 * q + 1, 1).wait_recv()
+            halo(2 * turn_no, 1).wait_recv()
+            halo(2 * turn_no + 1, 1).wait_recv()
 
         @pl.when(band > 0)
         def _():
-            halo(2 * q, 0).wait_recv()
-            halo(2 * q + 1, 0).wait_recv()
+            halo(2 * turn_no, 0).wait_recv()
+            halo(2 * turn_no + 1, 0).wait_recv()
+
+        return lax.fori_loop(2 * turn_no, 2 * turn_no + 2, one_visit, carry)
+
+    def weigh_pair(turn_no, carry):
+        arrived(turn_no + 3)
+        return lax.fori_loop(2 * turn_no, 2 * turn_no + 2, weigh, carry)
 
     share_edges(0)
-    share_edges(1)
-    wait_edges(0)
-    wait_edges(1)
-    lax.fori_loop(0, 3, one_visit, 0)
-    share_edges(2)
-    lax.fori_loop(3, 4, one_visit, 0)
-    wait_edges(2)
-    lax.fori_loop(4, 6, one_visit, 0)
+    lax.fori_loop(0, 3, filter_pair, 0)
+    lax.fori_loop(0, 3, weigh_pair, 0)
     o_ref[...] = num[...] / den[...]
 
     @pl.when(band < bands - 1)
@@ -343,20 +425,24 @@
         for visit in range(VISITS):
             halo(visit, 1).wait_send()
 
-    pltpu.make_async_copy(keys.at[pl.ds(0, n - 1)], keys.at[pl.ds(0, n - 1)], sk).wait()
-    for q in range(ROUNDS):
-        owner = q % 2
-        sent = rows.at[pl.ds(0, chips - 1)]
-        pltpu.make_async_copy(sent, sent, s1.at[q]).wait()
-
-        @pl.when(core != owner)
+    told = keys.at[0, pl.ds(0, zs - 1)]
+    pltpu.make_async_copy(told, told, sk).wait()
+    for d in range(1, 4):
+        forward(d).wait_send()
+    for visit in range(VISITS):
+        gone = rows.at[pl.ds(0, zs - 1)]
+        pltpu.make_async_copy(gone, gone, s1.at[visit]).wait()
+
+        @pl.when(lane4 != (visit % 2) * 2 + (visit // 2) % 2)
         def _():
-            pltpu.make_async_copy(rows.at[0], rows.at[0], s1b.at[q]).wait()
-
-        @pl.when(core == owner)
-        def _():
-            relayed = z.at[q, pl.ds(0, n - 1)]
-            pltpu.make_async_copy(relayed, relayed, s2.at[q]).wait()
+            pltpu.make_async_copy(rows.at[0], rows.at[0], s1b.at[visit]).wait()
+
+    relayed = z.at[0, pl.ds(0, n - 1)]
+    pltpu.make_async_copy(relayed, relayed, s2.at[0]).wait()
+
+    @pl.when(core == 0)
+    def _():
+        pltpu.make_async_copy(relayed, relayed, s2.at[1]).wait()
 
 
 def orders():
@@ -402,25 +488,29 @@
             vmem((128, 128), jnp.bfloat16),
             vmem((VISITS * 16, 16, 128), jnp.bfloat16),
             vmem((1, 128), jnp.float32),
-            vmem((ROUNDS, n, 16, 128), jnp.bfloat16),
-            vmem((n, 1, 128), jnp.float32),
-            vmem((ROUNDS, n, 2, 8, 128), jnp.bfloat16),
+            vmem((2, n, 16, 128), jnp.bfloat16),
+            vmem((4, n // 4, 1, 128), jnp.float32),
+            vmem((2, n, 2, 8, 128), jnp.bfloat16),
             vmem((VISITS * 16, 2, 8, 128), jnp.bfloat16),
             vmem((VISITS, 2, 8, 8, 128), jnp.bfloat16),
             vmem((256, WIDE), jnp.bfloat16),
             vmem((ROWS, DEPTH), jnp.float32),
             vmem((VISITS * 8, DEPTH), jnp.float32),
             vmem((DEPTH, COLS), jnp.bfloat16),
+            vmem((VISITS, ROWS, COLS), jnp.float32),
             vmem((ROWS, COLS), jnp.float32),
             vmem((ROWS, COLS), jnp.float32),
             dma((8,)),
-            dma((ROUNDS,)),
-            dma((ROUNDS,)),
-            dma((ROUNDS,)),
+            pltpu.SemaphoreType.REGULAR((len(LEVELS),)),
+            dma((VISITS,)),
+            dma((VISITS,)),
+            dma((2,)),
             dma,
             dma,
-            dma((ROUNDS,)),
-            dma((ROUNDS,)),
+            dma((3,)),
+            dma((3,)),
+            dma((2,)),
+            dma((VISITS,)),
             dma((VISITS, 2)),
             dma((VISITS, 2)),
         ],

time: 67.9 us -> 64 us (0.943)
  Pallas kernels: 65.3 us -> 61.9 us
    pallas_call x1, Pallas kernels: 65.3 us -> 61.9 us  [per_device(): pl.pallas_call(kernel, out_shape=jax.ShapeDtypeStruct((ROWS, COLS), jnp.f...]
where the time goes in v3:
time: 64 us; the launch traced here: 63.4 us
  Pallas kernels  61.9 us (97%)
  local copies, waits for them, and re-layouts  1.47 us (2%)
    pallas_call x1, Pallas kernels, per_device(): pl.pallas_call(kernel, out_shape=jax.ShapeDtypeStruct((ROWS, COLS), jnp.f...  61.9 us
    unnamed x1, local copies, waits for them, and re-layouts  1.47 us

profile of v3, /device:TPU:6, one launch (start us, length us, event | category | flops | bytes accessed | tf_op | source)
XLA Modules:
  0.0 63.4 jit_solution(18418815632631699144)
XLA Ops:
  0.0 61.9 %coadd.1 = f32[32,512]{1,0:T(8,128)} custom-call(bf16[6,16,8,128]{3,2,1,0:T(8,128)(2,1)} %flux_hbm.1, bf16[6,16,8,128]{3,2,1,0:T(8,128)(2,1)} %weight_hbm.1, s32[6,16]{1,0:T(8,128)} %patch_hbm.1, s32[6,16]{1,0:T(8,128)} %block_hbm.1, bf16[21,2,31]{2,1,0:T(2,128)(2,1)} %bitcast.4, f32[6,3,1,21]{3,2,1,0:T(1,128)} %bitcast.5, ...), custom_call_target="tpu_custom_call" | custom-call | tf_op jit(solution)/shard_map/coadd/pallas_call | solution.py:476
  61.9 1.5 %copy.10 = f32[1,32,512]{2,1,0:T(8,128)} copy(f32[1,32,512]{2,1,0:T(8,128)} %bitcast.3) | data formatting | bytes 131072

commit v4 on v3

--- a/solution.py
+++ b/solution.py
@@ -15,6 +15,7 @@
 NEAR = 4
 AHEAD = 3
 ROUNDS = 6
+P1ORDER = (0, 1, 2, 4, 5, 3)
 LEVELS = ((4, 0), (0, ROUNDS))
 PAIRS = (BASIS + 1) // 2
 DEPTH = PAIRS * 128
@@ -132,8 +133,13 @@
             device_id_type=MESH,
         ).start()
 
+    def place_of(turn_no, at):
+        if turn_no in (2, 3):
+            return (at + turn_no) % 2 * 2 + 1
+        return turn_no % 2 * 2
+
     def send_row(turn_no, step):
-        place = (turn_no % 2) * 2 + (turn_no // 2) % 2
+        place = place_of(turn_no, height + step + zs)
         pltpu.make_async_remote_copy(
             rows.at[turn_no * 16 + (height + step + zs) % zs],
             y.at[turn_no // 4, me],
@@ -164,7 +170,7 @@
 
     def own_height(rounds):
         for turn_no in rounds:
-            place = (turn_no % 2) * 2 + (turn_no // 2) % 2
+            place = place_of(turn_no, height)
 
             @pl.when(lane4 == place)
             def _():
@@ -200,7 +206,7 @@
             own_height(range(ROUNDS))
             sent = [known] * AHEAD + [0] * (ROUNDS - AHEAD)
         else:
-            for turn_no in range(count):
+            for turn_no in P1ORDER[:count]:
                 send_ring(sent[turn_no], known, (turn_no,), sent[turn_no] == before and turn_no == 0)
                 sent[turn_no] = known
         before = known
@@ -240,13 +246,21 @@
         ctable[0:128, span] = bf16(jnp.where(near, cyclic, 0.0))
         ctable[128:256, span] = bf16(jnp.where(near, 0.0, cyclic))
     ctable[:, BASIS * 128 :] = jnp.zeros((256, WIDE - BASIS * 128), jnp.bfloat16)
+    was, now = iota((128, 128), 0), iota((128, 128), 1)
+    inside = (was % 64 >= 16) & (was % 64 < 48)
+    moved_to = was // 64 * 32 + jnp.where(
+        inside, was % 64 - 16, 64 + jnp.where(was % 64 < 16, was % 64, was % 64 - 32)
+    )
+    regroup = one_hot(moved_to == now)
     for pair in range(PAIRS):
         taps = rbase[0][4 * pair + 1 : 4 * pair + 2]
         if 2 * pair + 1 < BASIS:
             taps = taps + rbase[1][4 * pair + 3 : 4 * pair + 4]
         taps = jnp.broadcast_to(taps, (ROWS, 128))
-        rtable[:, pair * 128 : (pair + 1) * 128] = pltpu.roll(taps, 0, 1, stride=1, stride_axis=0)
-    widen = one_hot(iota((BASIS, DEPTH), 0) == iota((BASIS, DEPTH), 1) // 64)
+        shifted = bf16(pltpu.roll(taps, 0, 1, stride=1, stride_axis=0))
+        rtable[:, pair * 128 : (pair + 1) * 128] = exact_dot(shifted, regroup)
+    column_basis = iota((BASIS, DEPTH), 1) // 128 * 2 + iota((BASIS, DEPTH), 1) % 64 // 32
+    widen = one_hot(iota((BASIS, DEPTH), 0) == column_basis)
     for visit in range(VISITS):
         for term in range(3):
             coefs[visit * 8 + term : visit * 8 + term + 1, 0:BASIS] = spatial[visit, term]
@@ -267,8 +281,11 @@
         half = (i + 1) // 2
         return n // 2 + half * (1 - 2 * (i % 2))
 
-    def relay(slot):
-        turn_no = me // 2 % 2 + 2 * core if slot == 0 else me // 2 % 2 + 4
+    side = me // 2 % 2
+    owned = ((1 - core) * side + core * (2 + (side + height) % 2), 4 + side)
+
+    def arrange(slot):
+        turn_no = owned[slot]
         visit = 2 * (turn_no % 3) + height // 8
         table = keys[...].reshape(64, 128)
         patch_of = jnp.floor(table * (1.0 / 16.0))
@@ -295,6 +312,9 @@
             moved = exact_dot(chosen, data)
             z[slot, part * 16 : (part + 1) * 16] = bf16(moved.reshape(16, 2, 8, 128))
 
+    def hand_out(slot):
+        turn_no = owned[slot]
+
         def send_blocks(i, carry):
             peer = (me + partner(i)) % n
             pltpu.make_async_remote_copy(
@@ -310,11 +330,16 @@
         lax.fori_loop(0, n - 1, send_blocks, 0)
         pltpu.make_async_copy(z.at[slot, me], g.at[turn_no * 16 + height], r2.at[turn_no]).start()
 
-    relay(0)
+    arrange(0)
+
+    @pl.when(owned[0] != 3)
+    def _():
+        hand_out(0)
 
     @pl.when(core == 0)
     def _():
-        relay(1)
+        arrange(1)
+        hand_out(1)
 
     def halo(visit, side):
         half, step = (1, 1) if side == 0 else (0, -1)
@@ -332,45 +357,76 @@
     w = (2.0 * iota((1, COLS), 1).astype(jnp.float32) + 1.0) / COLS - 1.0
     above_on = jnp.broadcast_to(band, (8, 128)) > 0
     below_on = jnp.broadcast_to(band, (8, 128)) < bands - 1
-    left_lane = iota((256, 128), 1) < 64
-
-    def one_visit(visit, carry):
-        unit = visit * 8
-        above = [jnp.where(above_on, h[visit, 0, r].astype(jnp.float32), 0.0) for r in range(8)]
-        below = [jnp.where(below_on, h[visit, 1, r].astype(jnp.float32), 0.0) for r in range(8)]
-        inner = [g[unit + r, half].astype(jnp.float32) for r in range(8) for half in range(2)]
-        image = bf16(jnp.concatenate(above + inner + below, axis=0))
-        moved = exact_dot(order[...], image)
-        beside = jnp.where(left_lane, moved[256:512], moved[512:768])
-        window = bf16(jnp.concatenate([moved[0:256], beside], axis=1))
+    left_lane = iota((128, 256), 1) % 128 < 64
+
+    def filter_columns(turn_no, part):
+        images = []
+        for k in range(2):
+            visit = 2 * turn_no + k
+            if part == 0:
+                blocks = [
+                    g[visit * 8 + r, half].astype(jnp.float32) for r in range(8) for half in range(2)
+                ]
+            else:
+                blocks = [
+                    jnp.where(on, h[visit, place, r].astype(jnp.float32), 0.0)
+                    for place, on in ((0, above_on), (1, below_on))
+                    for r in range(8)
+                ]
+            images.append(bf16(jnp.concatenate(blocks, axis=0)))
+        moved = exact_dot(order[part], jnp.concatenate(images, axis=1))
+        beside = jnp.where(left_lane, moved[128:256], moved[256:384])
+        window = jnp.concatenate(
+            [
+                jnp.concatenate([half[0:128, k * 128 : (k + 1) * 128] for half in (moved, beside)], 1)
+                for k in range(2)
+            ],
+            axis=0,
+        )
+        window = bf16(window)
         for pair in range(PAIRS):
             result = bf16(exact_dot(window, ctable[:, pair * 256 : (pair + 1) * 256]))
-            for odd in range(2):
-                b = 2 * pair + odd
-                for c in range(4):
-                    filtered[b * 64 : (b + 1) * 64, c * 128 : (c + 1) * 128] = result[
-                        c * 64 : (c + 1) * 64, odd * 128 : (odd + 1) * 128
-                    ]
-        coef = coefs[pl.ds(pl.multiple_of(visit * 8, 8), 8)]
-        table = rtable[...]
-        steady = table * (coef[0:1] + u * coef[1:2])
-        slope = table * coef[2:3]
-        full = jnp.concatenate([steady, slope], axis=0)
-        high = bf16(full)
-        low = bf16(full - high.astype(jnp.float32))
-        mixed = exact_dot(jnp.concatenate([high, low], axis=0), filtered[...])
-        mixed = mixed[0:64] + mixed[64:128]
-        matched[visit] = mixed[0:ROWS] + w * mixed[ROWS:64]
-        return carry
-
-    def weigh(visit, carry):
-        unit = (VISITS + visit) * 8
-        weights = [g[unit + r, half].astype(jnp.float32) for r in range(8) for half in range(2)]
-        weights = exact_dot(worder[...], bf16(jnp.concatenate(weights, axis=0)))
-        weights = jnp.concatenate([weights[c * ROWS : (c + 1) * ROWS] for c in range(4)], axis=1)
-        num[...] += weights * matched[visit]
-        den[...] += weights
-        return carry
+            for k in range(2):
+                for odd in range(2):
+                    at = pair * 128 + part * 64 + odd * 32
+                    for c in range(4):
+                        filtered[turn_no, k, at : at + 32, c * 128 : (c + 1) * 128] = result[
+                            k * 128 + c * 32 : k * 128 + (c + 1) * 32,
+                            odd * 128 : (odd + 1) * 128,
+                        ]
+
+    def mix_rows(turn_no):
+        for k in range(2):
+            visit = 2 * turn_no + k
+            coef = coefs[pl.ds(pl.multiple_of(visit * 8, 8), 8)]
+            table = rtable[...]
+            steady = table * (coef[0:1] + u * coef[1:2])
+            slope = table * coef[2:3]
+            full = jnp.concatenate([steady, slope], axis=0)
+            high = bf16(full)
+            low = bf16(full - high.astype(jnp.float32))
+            mixed = exact_dot(jnp.concatenate([high, low], axis=0), filtered[turn_no, k])
+            mixed = mixed[0:64] + mixed[64:128]
+            matched[visit] = mixed[0:ROWS] + w * mixed[ROWS:64]
+
+    def weigh_two(turn_no):
+        pixels = []
+        for k in range(2):
+            unit = (VISITS + 2 * turn_no + k) * 8
+            pixels.append(
+                jnp.concatenate(
+                    [g[unit + r, half].astype(jnp.float32) for r in range(8) for half in range(2)], 0
+                )
+            )
+        turned = exact_dot(worder[...], bf16(jnp.concatenate(pixels, axis=1)))
+        top, bottom = num[...], den[...]
+        for k in range(2):
+            weights = jnp.concatenate(
+                [turned[c * ROWS : (c + 1) * ROWS, k * 128 : (k + 1) * 128] for c in range(4)], axis=1
+            )
+            top += weights * matched[2 * turn_no + k]
+            bottom += weights
+        num[...], den[...] = top, bottom
 
     def arrived(turn_no):
         part = g.at[pl.ds(turn_no * 16, 16)]
@@ -389,10 +445,8 @@
             halo(2 * turn_no, 1).start()
             halo(2 * turn_no + 1, 1).start()
 
-    def filter_pair(turn_no, carry):
-        @pl.when(turn_no < 2)
-        def _():
-            share_edges(turn_no + 1)
+    def filter_pair(i, carry):
+        turn_no = (i + 2) % 3
 
         @pl.when(band < bands - 1)
         def _():
@@ -404,13 +458,31 @@
             halo(2 * turn_no, 0).wait_recv()
             halo(2 * turn_no + 1, 0).wait_recv()
 
-        return lax.fori_loop(2 * turn_no, 2 * turn_no + 2, one_visit, carry)
-
-    def weigh_pair(turn_no, carry):
+        filter_columns(turn_no, 1)
+        mix_rows(turn_no)
+        return carry
+
+    def weigh_pair(i, carry):
+        turn_no = (i + 1) % 3
         arrived(turn_no + 3)
-        return lax.fori_loop(2 * turn_no, 2 * turn_no + 2, weigh, carry)
-
+        weigh_two(turn_no)
+        return carry
+
+    share_edges(2)
+
+    @pl.when(owned[0] == 3)
+    def _():
+        hand_out(0)
+
+    filter_columns(2, 0)
     share_edges(0)
+    share_edges(1)
+
+    def filter_inner(turn_no, carry):
+        filter_columns(turn_no, 0)
+        return carry
+
+    lax.fori_loop(0, 2, filter_inner, 0)
     lax.fori_loop(0, 3, filter_pair, 0)
     lax.fori_loop(0, 3, weigh_pair, 0)
     o_ref[...] = num[...] / den[...]
@@ -433,7 +505,7 @@
         gone = rows.at[pl.ds(0, zs - 1)]
         pltpu.make_async_copy(gone, gone, s1.at[visit]).wait()
 
-        @pl.when(lane4 != (visit % 2) * 2 + (visit // 2) % 2)
+        @pl.when(lane4 != place_of(visit, height))
         def _():
             pltpu.make_async_copy(rows.at[0], rows.at[0], s1b.at[visit]).wait()
 
@@ -466,7 +538,10 @@
     for c in range(4):
         for s in range(ROWS):
             worder[c, s, (s % 8) * 16 + (s // 8) * 4 + c] = 1.0
-    return order.reshape(768, 256), worder.reshape(128, 128)
+    inner = order[:, :, 16:48, 64:192].reshape(384, 128)
+    outer = np.concatenate([order[:, :, :16], order[:, :, 48:]], axis=2)
+    outer = np.concatenate([outer[..., :64], outer[..., 192:]], axis=3).reshape(384, 128)
+    return np.stack([inner, outer]), worder.reshape(128, 128)
 
 
 def per_device(tile_flux, tile_weight, dest_patch, dest_block, basis, spatial):
@@ -475,7 +550,7 @@
     order, worder = orders()
     coadd = pl.pallas_call(
         kernel,
-        out_shape=jax.ShapeDtypeStruct((ROWS, COLS), jnp.float32),
+        out_shape=vmem((ROWS, COLS), jnp.float32),
         in_specs=[pl.BlockSpec(memory_space=pl.ANY)] * 8,
         out_specs=pl.BlockSpec(memory_space=vmem),
         scratch_shapes=[
@@ -484,7 +559,7 @@
             vmem((BASIS, 2, TAPS), jnp.bfloat16),
             vmem((VISITS, 3, 1, BASIS), jnp.float32),
             vmem((48, 128), jnp.float32),
-            vmem((768, 256), jnp.bfloat16),
+            vmem((2, 384, 128), jnp.bfloat16),
             vmem((128, 128), jnp.bfloat16),
             vmem((VISITS * 16, 16, 128), jnp.bfloat16),
             vmem((1, 128), jnp.float32),
@@ -496,7 +571,7 @@
             vmem((256, WIDE), jnp.bfloat16),
             vmem((ROWS, DEPTH), jnp.float32),
             vmem((VISITS * 8, DEPTH), jnp.float32),
-            vmem((DEPTH, COLS), jnp.bfloat16),
+            vmem((3, 2, DEPTH, COLS), jnp.bfloat16),
             vmem((VISITS, ROWS, COLS), jnp.float32),
             vmem((ROWS, COLS), jnp.float32),
             vmem((ROWS, COLS), jnp.float32),

time: 64 us -> 58.1 us (0.908)
  Pallas kernels: 61.9 us -> 57.3 us
  local copies, waits for them, and re-layouts: 1.47 us -> 0.63 us
    pallas_call x1, Pallas kernels: 61.9 us -> 57.3 us  [per_device(): pl.pallas_call(kernel, out_shape=vmem((ROWS, COLS), jnp.float32), in_spec...]
    unnamed x1, local copies, waits for them, and re-layouts: 1.47 us -> 0.63 us
where the time goes in v4:
time: 58.1 us; the launch traced here: 58 us
  Pallas kernels  57.3 us (99%)
  local copies, waits for them, and re-layouts  0.63 us (1%)
    pallas_call x1, Pallas kernels, per_device(): pl.pallas_call(kernel, out_shape=vmem((ROWS, COLS), jnp.float32), in_spec...  57.3 us

profile of v4, /device:TPU:6, one launch (start us, length us, event | category | flops | bytes accessed | tf_op | source)
XLA Modules:
  0.0 58.0 jit_solution(12709769590766176050)
XLA Ops:
  0.0 57.3 %coadd.1 = f32[32,512]{1,0:T(8,128)S(1)} custom-call(bf16[6,16,8,128]{3,2,1,0:T(8,128)(2,1)} %flux_hbm.1, bf16[6,16,8,128]{3,2,1,0:T(8,128)(2,1)} %weight_hbm.1, s32[6,16]{1,0:T(8,128)} %patch_hbm.1, s32[6,16]{1,0:T(8,128)} %block_hbm.1, bf16[21,2,31]{2,1,0:T(2,128)(2,1)} %bitcast.4, f32[6,3,1,21]{3,2,1,0:T(1,128)} %bitcast.5, ...), custom_call_target="tpu_custom_call" | custom-call | tf_op jit(solution)/shard_map/coadd/pallas_call | solution.py:551
  57.3 0.6 %copy.10 = f32[1,32,512]{2,1,0:T(8,128)} copy(f32[1,32,512]{2,1,0:T(8,128)S(1)} %bitcast.3) | data formatting | bytes 131072

commit v5 on v4

--- a/solution.py
+++ b/solution.py
@@ -40,7 +40,7 @@
 
 def kernel(flux_hbm, weight_hbm, patch_hbm, block_hbm, basis_hbm, spatial_hbm, order_hbm, worder_hbm,
            o_ref, tiles, dest, basis, spatial, both, order, worder, rows, key_row, y, keys, z, g, h,
-           ctable, rtable, coefs, filtered, matched, num, den,
+           ctable, rtable, coefs, blend, filtered, matched, num, den,
            load, heard, s1, s1b, r1, sk, rk, sk4, rk4, s2, r2, sh, rh):
     n, bands = lax.axis_size("patch"), lax.axis_size("band")
     me, band = lax.axis_index("patch"), lax.axis_index("band")
@@ -271,6 +271,21 @@
     middle = bf16(rest)
     bottom = bf16(rest - middle.astype(jnp.float32))
     coefs[...] = exact_dot(top, widen) + exact_dot(middle, widen) + exact_dot(bottom, widen)
+    first = (band * ROWS).astype(jnp.float32)
+    u = (2.0 * (iota((ROWS, 1), 0).astype(jnp.float32) + first) + 1.0) / (bands * ROWS) - 1.0
+
+    def fill_blend(visit, carry):
+        coef = coefs[pl.ds(pl.multiple_of(visit * 8, 8), 8)]
+        table = rtable[...]
+        steady = table * (coef[0:1] + u * coef[1:2])
+        slope = table * coef[2:3]
+        full = jnp.concatenate([steady, slope], axis=0)
+        high = bf16(full)
+        low = bf16(full - high.astype(jnp.float32))
+        blend[visit] = jnp.concatenate([high, low], axis=0)
+        return carry
+
+    lax.fori_loop(0, VISITS, fill_blend, 0)
     num[...] = jnp.zeros_like(num)
     den[...] = jnp.zeros_like(den)
 
@@ -341,19 +356,17 @@
         arrange(1)
         hand_out(1)
 
-    def halo(visit, side):
+    def halo(turn_no, side):
         half, step = (1, 1) if side == 0 else (0, -1)
         return pltpu.make_async_remote_copy(
-            g.at[pl.ds(visit * 8, 8), half],
-            h.at[visit, side],
-            sh.at[visit, side],
-            rh.at[visit, side],
+            g.at[pl.ds(turn_no * 16, 16), half],
+            h.at[turn_no, side],
+            sh.at[turn_no, side],
+            rh.at[turn_no, side],
             device_id={"band": band + step},
             device_id_type=MESH,
         )
 
-    first = (band * ROWS).astype(jnp.float32)
-    u = (2.0 * (iota((ROWS, 1), 0).astype(jnp.float32) + first) + 1.0) / (bands * ROWS) - 1.0
     w = (2.0 * iota((1, COLS), 1).astype(jnp.float32) + 1.0) / COLS - 1.0
     above_on = jnp.broadcast_to(band, (8, 128)) > 0
     below_on = jnp.broadcast_to(band, (8, 128)) < bands - 1
@@ -369,7 +382,7 @@
                 ]
             else:
                 blocks = [
-                    jnp.where(on, h[visit, place, r].astype(jnp.float32), 0.0)
+                    jnp.where(on, h[turn_no, place, k * 8 + r].astype(jnp.float32), 0.0)
                     for place, on in ((0, above_on), (1, below_on))
                     for r in range(8)
                 ]
@@ -398,14 +411,7 @@
     def mix_rows(turn_no):
         for k in range(2):
             visit = 2 * turn_no + k
-            coef = coefs[pl.ds(pl.multiple_of(visit * 8, 8), 8)]
-            table = rtable[...]
-            steady = table * (coef[0:1] + u * coef[1:2])
-            slope = table * coef[2:3]
-            full = jnp.concatenate([steady, slope], axis=0)
-            high = bf16(full)
-            low = bf16(full - high.astype(jnp.float32))
-            mixed = exact_dot(jnp.concatenate([high, low], axis=0), filtered[turn_no, k])
+            mixed = exact_dot(blend[visit], filtered[turn_no, k])
             mixed = mixed[0:64] + mixed[64:128]
             matched[visit] = mixed[0:ROWS] + w * mixed[ROWS:64]
 
@@ -437,26 +443,22 @@
 
         @pl.when(band < bands - 1)
         def _():
-            halo(2 * turn_no, 0).start()
-            halo(2 * turn_no + 1, 0).start()
+            halo(turn_no, 0).start()
 
         @pl.when(band > 0)
         def _():
-            halo(2 * turn_no, 1).start()
-            halo(2 * turn_no + 1, 1).start()
+            halo(turn_no, 1).start()
 
     def filter_pair(i, carry):
         turn_no = (i + 2) % 3
 
         @pl.when(band < bands - 1)
         def _():
-            halo(2 * turn_no, 1).wait_recv()
-            halo(2 * turn_no + 1, 1).wait_recv()
+            halo(turn_no, 1).wait_recv()
 
         @pl.when(band > 0)
         def _():
-            halo(2 * turn_no, 0).wait_recv()
-            halo(2 * turn_no + 1, 0).wait_recv()
+            halo(turn_no, 0).wait_recv()
 
         filter_columns(turn_no, 1)
         mix_rows(turn_no)
@@ -489,13 +491,13 @@
 
     @pl.when(band < bands - 1)
     def _():
-        for visit in range(VISITS):
-            halo(visit, 0).wait_send()
+        for turn_no in range(3):
+            halo(turn_no, 0).wait_send()
 
     @pl.when(band > 0)
     def _():
-        for visit in range(VISITS):
-            halo(visit, 1).wait_send()
+        for turn_no in range(3):
+            halo(turn_no, 1).wait_send()
 
     told = keys.at[0, pl.ds(0, zs - 1)]
     pltpu.make_async_copy(told, told, sk).wait()
@@ -567,10 +569,11 @@
             vmem((4, n // 4, 1, 128), jnp.float32),
             vmem((2, n, 2, 8, 128), jnp.bfloat16),
             vmem((VISITS * 16, 2, 8, 128), jnp.bfloat16),
-            vmem((VISITS, 2, 8, 8, 128), jnp.bfloat16),
+            vmem((3, 2, 16, 8, 128), jnp.bfloat16),
             vmem((256, WIDE), jnp.bfloat16),
             vmem((ROWS, DEPTH), jnp.float32),
             vmem((VISITS * 8, DEPTH), jnp.float32),
+            vmem((VISITS, 4 * ROWS, DEPTH), jnp.bfloat16),
             vmem((3, 2, DEPTH, COLS), jnp.bfloat16),
             vmem((VISITS, ROWS, COLS), jnp.float32),
             vmem((ROWS, COLS), jnp.float32),
@@ -586,8 +589,8 @@
             dma((3,)),
             dma((2,)),
             dma((VISITS,)),
-            dma((VISITS, 2)),
-            dma((VISITS, 2)),
+            dma((3, 2)),
+            dma((3, 2)),
         ],
         compiler_params=pltpu.CompilerParams(collective_id=0, has_side_effects=True),
         name="coadd",

time: 58.1 us -> 57.9 us (level)
  no operation moved by 1% of the time
where the time goes in v5:
time: 57.9 us; the launch traced here: 57.8 us
  Pallas kernels  57.2 us (99%)
  local copies, waits for them, and re-layouts  0.63 us (1%)
    pallas_call x1, Pallas kernels, per_device(): pl.pallas_call(kernel, out_shape=vmem((ROWS, COLS), jnp.float32), in_spec...  57.2 us

profile of v5, /device:TPU:6, one launch (start us, length us, event | category | flops | bytes accessed | tf_op | source)
XLA Modules:
  0.0 57.8 jit_solution(1957718072727714210)
XLA Ops:
  0.0 57.2 %coadd.1 = f32[32,512]{1,0:T(8,128)S(1)} custom-call(bf16[6,16,8,128]{3,2,1,0:T(8,128)(2,1)} %flux_hbm.1, bf16[6,16,8,128]{3,2,1,0:T(8,128)(2,1)} %weight_hbm.1, s32[6,16]{1,0:T(8,128)} %patch_hbm.1, s32[6,16]{1,0:T(8,128)} %block_hbm.1, bf16[21,2,31]{2,1,0:T(2,128)(2,1)} %bitcast.4, f32[6,3,1,21]{3,2,1,0:T(1,128)} %bitcast.5, ...), custom_call_target="tpu_custom_call" | custom-call | tf_op jit(solution)/shard_map/coadd/pallas_call | solution.py:553
  57.2 0.6 %copy.10 = f32[1,32,512]{2,1,0:T(8,128)} copy(f32[1,32,512]{2,1,0:T(8,128)S(1)} %bitcast.3) | data formatting | bytes 131072

commit v6 on v5

--- a/solution.py
+++ b/solution.py
@@ -477,10 +477,8 @@
         hand_out(0)
 
     filter_columns(2, 0)
-    share_edges(0)
-    share_edges(1)
-
     def filter_inner(turn_no, carry):
+        share_edges(turn_no)
         filter_columns(turn_no, 0)
         return carry
 

time: 57.9 us -> 57.9 us (level)
  no operation moved by 1% of the time
where the time goes in v6:
time: 57.9 us; the launch traced here: 57.8 us
  Pallas kernels  57.2 us (99%)
  local copies, waits for them, and re-layouts  0.63 us (1%)
    pallas_call x1, Pallas kernels, per_device(): pl.pallas_call(kernel, out_shape=vmem((ROWS, COLS), jnp.float32), in_spec...  57.2 us

profile of v6, /device:TPU:6, one launch (start us, length us, event | category | flops | bytes accessed | tf_op | source)
XLA Modules:
  0.0 57.8 jit_solution(14362675683919607163)
XLA Ops:
  0.0 57.2 %coadd.1 = f32[32,512]{1,0:T(8,128)S(1)} custom-call(bf16[6,16,8,128]{3,2,1,0:T(8,128)(2,1)} %flux_hbm.1, bf16[6,16,8,128]{3,2,1,0:T(8,128)(2,1)} %weight_hbm.1, s32[6,16]{1,0:T(8,128)} %patch_hbm.1, s32[6,16]{1,0:T(8,128)} %block_hbm.1, bf16[21,2,31]{2,1,0:T(2,128)(2,1)} %bitcast.4, f32[6,3,1,21]{3,2,1,0:T(1,128)} %bitcast.5, ...), custom_call_target="tpu_custom_call" | custom-call | tf_op jit(solution)/shard_map/coadd/pallas_call | solution.py:551
  57.2 0.6 %copy.10 = f32[1,32,512]{2,1,0:T(8,128)} copy(f32[1,32,512]{2,1,0:T(8,128)S(1)} %bitcast.3) | data formatting | bytes 131072
